TPU v7x, 128 devices: a whole 4x4x4 slice. The times are simulated.
128 devices in a mesh: tok: 16 (over x, y), head: 8 (over z, core).
Axes of the slice: x: 4, y: 4, z: 4, core: 2. Of those that a mesh axis runs over, the one named last changes fastest.
Arguments:
- tokens: bfloat16 [16384, 1536], P(('tok', 'head')), may hold values from -6 to 6
- segments: int32 [16384], replicated, may hold values from 0 to 127, never falling along the last dimension, each value on 1 to 1024 neighbouring positions
- group_ids: int32 [128], replicated, may hold values from 0 to 15
- prefix_owner: int32 [16], replicated, may hold values from 0 to 15, each once
- slab_fill: int32 [16], replicated, may hold values from 256 to 512
- prefix_cache: bfloat16 [8192, 1024], P('tok', 'head'), may hold values from -400 to 400, as said below
- attn_gain: float32 [1536], replicated, may hold values from 0.5 to 1.5
- w_query: bfloat16 [1536, 1536], P(None, 'head'), may hold values from -0.15625 to 0.15625
- w_keyval: bfloat16 [1536, 1024], P(None, 'head'), may hold values from -0.15625 to 0.15625
- w_out: bfloat16 [1536, 1536], P('head'), may hold values from -0.15625 to 0.15625
- ffn_gain: float32 [1536], replicated, may hold values from 0.5 to 1.5
- routes: int32 [16384, 8], P(('tok', 'head')), may hold values from 0 to 31, all different within a row; in each aligned block of 128 rows (0 to 127, 128 to 255, ...) at most 64 rows name the same one
- route_gates: float32 [16384, 8], P(('tok', 'head')), may hold values from 0.05 to 0.5
- w_gate: bfloat16 [32, 1536, 512], P('tok'), may hold values from -0.15625 to 0.15625
- w_up: bfloat16 [32, 1536, 512], P('tok'), may hold values from -0.15625 to 0.15625
- w_down: bfloat16 [32, 512, 1536], P('tok'), may hold values from -0.25 to 0.25
Outputs:
- layer_out: bfloat16 [16384, 1536], P(('tok', 'head'))
Inputs may be any that keep to these rules, and one draw needn't show every extreme that they name: `segments`: request ids never fall along the tokens; every request has 1 to 1024 tokens and some request exactly 1024. `prefix_owner`: each group's prefix lies in exactly one slab. `prefix_cache`: keys are already rotated by their positions 0 to fill - 1; rows at fill and past it are padding. `routes`: each row names 8 different experts; the rows of one device name any expert at most 64 times.
All inputs are finite; a program needn't handle non-finite values.
Results may differ from a plain program's by a relative error of at most 0.012.
Values may be sent and summed in bfloat16 or wider, within the bound.
A program may use at most 192 MiB of HBM per device.

v0:
```python
import jax
import jax.numpy as jnp
from jax import lax
from jax.sharding import PartitionSpec as P

HS = 64
EXPERTS = 32
TOPK = 8
PREFIX = 512
CAP = 64


NEG_FILL = -1e30
NORM_EPS = 1e-06
key_block = 512


def shifted(block, axis, distance):
    devices = range(lax.axis_size(axis))
    route = [(i - distance, i) for i in devices if i - distance in devices]
    return lax.ppermute(block, axis, route)


def rms_scale(values, gain):
    widened = values.astype(jnp.float32)
    spread = jnp.mean(widened * widened, axis=-1, keepdims=True)
    return widened * lax.rsqrt(spread + NORM_EPS) * gain


def lookup(table, index):
    entries = jnp.arange(table.shape[0], dtype=jnp.int32)
    return jnp.sum(jnp.where(index[..., None] == entries, table, 0), axis=-1)


def token_tables(segments, group_ids, prefix_owner, slab_fill):
    length_all = segments.shape[0]
    places = jnp.arange(length_all, dtype=jnp.int32)
    opening = jnp.concatenate([jnp.ones((1,), dtype=bool), segments[1:] != segments[:-1]])
    begins = lax.cummax(jnp.where(opening, places, 0), axis=0)
    slab_ids = lookup(prefix_owner, lookup(group_ids, segments))
    token_fill = lookup(slab_fill, slab_ids)
    return (slab_ids, token_fill, token_fill + places - begins)


def rope_angles(positions, head_size):
    steps_idx = jnp.arange(head_size // 2, dtype=jnp.float32)
    inverse = jnp.exp(steps_idx * (-2.0 * jnp.log(10000.0) / head_size))
    return positions.astype(jnp.float32)[:, None] * inverse[None, :]


def rotate(values, angles):
    halfway = values.shape[-1] // 2
    leading = values[..., :halfway]
    trailing = values[..., halfway:]
    cosine = jnp.cos(angles)[:, None, :]
    sine_v = jnp.sin(angles)[:, None, :]
    return jnp.concatenate(
        [leading * cosine - trailing * sine_v, trailing * cosine + leading * sine_v], axis=-1
    )


def absorb(carry, query_heads, key_rows, value_rows, visible):
    peak_old, weight_sum, accum = carry
    scores = jnp.einsum(
        "qgrd,kgd->qgrk", query_heads, key_rows, preferred_element_type=jnp.float32
    ) * HS ** (-0.5)
    shown = visible[:, None, None, :]
    scores = jnp.where(shown, scores, NEG_FILL)
    peak_new = jnp.maximum(peak_old, jnp.max(scores, axis=-1))
    weights = jnp.where(shown, jnp.exp(scores - peak_new[..., None]), 0.0)
    factor = jnp.exp(peak_old - peak_new)
    weight_sum = weight_sum * factor + jnp.sum(weights, axis=-1)
    accum = accum * factor[..., None] + jnp.einsum(
        "qgrk,kgd->qgrd",
        weights.astype(jnp.bfloat16),
        value_rows,
        preferred_element_type=jnp.float32,
    )
    return (peak_new, weight_sum, accum)


def local(
    tokens,
    segments,
    group_ids,
    prefix_owner,
    slab_fill,
    prefix_cache,
    attn_gain,
    w_query,
    w_keyval,
    w_out,
    ffn_gain,
    routes,
    route_gates,
    w_gate,
    w_up,
    w_down,
):
    tok_count = lax.axis_size("tok")
    head_count = lax.axis_size("head")
    tok_place = lax.axis_index("tok")
    rows_dev = tokens.shape[0]
    row_len = rows_dev * head_count
    row_first = tok_place * row_len
    kv_local = w_keyval.shape[1] // (2 * HS)
    q_local = w_query.shape[1] // HS
    group_share = q_local // kv_local
    slab_ids, token_fill, positions = token_tables(segments, group_ids, prefix_owner, slab_fill)
    row_pos = lax.dynamic_slice_in_dim(positions, row_first, row_len, 0)
    row_segs = lax.dynamic_slice_in_dim(segments, row_first, row_len, 0)
    row_slab = lax.dynamic_slice_in_dim(slab_ids, row_first, row_len, 0)
    normed = rms_scale(tokens, attn_gain).astype(jnp.bfloat16)
    piece = lax.all_gather(normed, "head", axis=0, tiled=True)
    projected = jnp.concatenate(
        [
            jnp.dot(piece, w_query, preferred_element_type=jnp.float32),
            jnp.dot(piece, w_keyval, preferred_element_type=jnp.float32),
        ],
        axis=1,
    )
    angles = rope_angles(row_pos, HS)
    query_part = projected[:, : q_local * HS].reshape(row_len, q_local, HS)
    keyval = projected[:, q_local * HS :].reshape(row_len, kv_local, 2, HS)
    query_flat = rotate(query_part, angles).astype(jnp.bfloat16).reshape(row_len, q_local * HS)
    query_heads = query_flat.reshape(row_len, kv_local, group_share, HS)
    key_rows = rotate(keyval[:, :, 0], angles)
    kv_now = (
        jnp.stack([key_rows, keyval[:, :, 1]], axis=2)
        .astype(jnp.bfloat16)
        .reshape(row_len, kv_local * 2 * HS)
    )
    kv_prev = shifted(kv_now, "tok", 1)
    near = jnp.concatenate([kv_prev, kv_now], axis=0).reshape(2 * row_len, kv_local, 2, HS)
    segs_pad = jnp.concatenate([jnp.full((row_len,), -1, jnp.int32), segments], axis=0)
    near_segs = lax.dynamic_slice_in_dim(segs_pad, row_first, 2 * row_len, 0)
    near_pos = row_first - row_len + jnp.arange(2 * row_len, dtype=jnp.int32)
    query_pos = row_first + jnp.arange(row_len, dtype=jnp.int32)
    near_mask = (near_segs[None, :] == row_segs[:, None]) & (
        near_pos[None, :] <= query_pos[:, None]
    )
    start_carry = (
        jnp.full((row_len, kv_local, group_share), NEG_FILL, jnp.float32),
        jnp.zeros((row_len, kv_local, group_share), jnp.float32),
        jnp.zeros((row_len, kv_local, group_share, HS), jnp.float32),
    )
    carry = absorb(start_carry, query_heads, near[:, :, 0], near[:, :, 1], near_mask)

    def one_block(state, block_rows, first_row):
        where_rows = first_row + jnp.arange(block_rows.shape[0], dtype=jnp.int32)
        slab_of = where_rows // PREFIX
        inside = where_rows - slab_of * PREFIX
        limit_rows = lookup(slab_fill, slab_of)
        visible = (slab_of[None, :] == row_slab[:, None]) & (inside < limit_rows)[None, :]
        split_rows = block_rows.reshape(block_rows.shape[0], kv_local, 2, HS)
        return absorb(state, query_heads, split_rows[:, :, 0], split_rows[:, :, 1], visible)

    state = carry
    piece = lax.all_gather(prefix_cache, "tok", axis=0, tiled=True)
    length_rows = piece.shape[0]
    stacked = piece.reshape(length_rows // key_block, key_block, piece.shape[1])

    def advance(inner_state, entry_pair):
        return (one_block(inner_state, entry_pair[0], entry_pair[1] * key_block), None)

    state, _ = lax.scan(
        advance, state, (stacked, jnp.arange(length_rows // key_block, dtype=jnp.int32))
    )
    carry = state
    final_peak, final_sum, final_acc = carry
    mixed = (final_acc / final_sum[..., None]).reshape(row_len, q_local * HS).astype(jnp.bfloat16)
    attended = lax.psum_scatter(
        jnp.dot(mixed, w_out, preferred_element_type=jnp.float32).astype(jnp.bfloat16),
        "head",
        scatter_dimension=0,
        tiled=True,
    ).astype(jnp.float32)
    hidden = tokens.astype(jnp.float32) + attended
    expert_in = rms_scale(hidden, ffn_gain).astype(jnp.bfloat16)
    exp_local = w_gate.shape[0]
    flat_routes = routes.reshape(-1)
    route_count = flat_routes.shape[0]
    onehot = flat_routes[:, None] == jnp.arange(EXPERTS, dtype=jnp.int32)[None, :]
    ranks = jnp.sum(jnp.where(onehot, jnp.cumsum(onehot.astype(jnp.int32), axis=0) - 1, 0), axis=1)
    slot_of = flat_routes * CAP + ranks
    source_row = jnp.arange(route_count, dtype=jnp.int32) // TOPK
    slot_token = jnp.zeros((EXPERTS * CAP,), jnp.int32).at[slot_of].set(source_row)
    slot_used = jnp.zeros((EXPERTS * CAP,), jnp.bool_).at[slot_of].set(True)
    outgoing = jnp.where(slot_used[:, None], expert_in[slot_token], 0.0)
    outgoing = outgoing.reshape(tok_count, exp_local, CAP, expert_in.shape[1])
    arrived = lax.all_to_all(outgoing, "tok", split_axis=0, concat_axis=0, tiled=True)
    gate_val = jnp.einsum("secd,edf->secf", arrived, w_gate, preferred_element_type=jnp.float32)
    up_val = jnp.einsum("secd,edf->secf", arrived, w_up, preferred_element_type=jnp.float32)
    inner_act = (jax.nn.silu(gate_val) * up_val).astype(jnp.bfloat16)
    answered = jnp.einsum(
        "secf,efd->secd", inner_act, w_down, preferred_element_type=jnp.float32
    ).astype(jnp.bfloat16)
    returned = lax.all_to_all(answered, "tok", split_axis=0, concat_axis=0, tiled=True).reshape(
        EXPERTS * CAP, expert_in.shape[1]
    )
    per_route = returned[slot_of].reshape(rows_dev, TOPK, expert_in.shape[1])
    mixture = hidden
    for choice_rank in range(TOPK):
        mixture = mixture + route_gates[:, choice_rank, None] * per_route[:, choice_rank].astype(
            jnp.float32
        )
    return mixture.astype(jnp.bfloat16)


def solution(mesh):
    return jax.shard_map(
        local,
        mesh=mesh,
        in_specs=(
            P(("tok", "head"), None),
            P(),
            P(),
            P(),
            P(),
            P("tok", "head"),
            P(),
            P(None, "head"),
            P(None, "head"),
            P("head", None),
            P(),
            P(("tok", "head"), None),
            P(("tok", "head"), None),
            P("tok", None, None),
            P("tok", None, None),
            P("tok", None, None),
        ),
        out_specs=P(("tok", "head"), None),
        check_vma=False,
    )
```

profile of v0, /device:TPU:0, one launch (start us, length us, event | category | flops | bytes accessed | tf_op | source)
XLA Modules:
  0.0 665.5 jit_solution(6953487742649804318)
XLA Ops:
  7.9 1.9 fusion.60
  13.2 6.0 select_reduce_fusion.1
  22.9 3.3 compare_and_fusion.1
  26.2 14.1 %all-gather.3.cloned.1.call-done = bf16[1024,1536]{1,0:T(8,128)(2,1)} async-done(((bf16[128,1536]{1,0:T(8,128)(2,1)}), bf16[1024,1536]{1,0:T(8,128)(2,1)}) %all-gather.3.cloned.1.call-update) | async-done | bytes 3145744 | tf_op jit(solution)/shard_map/all_gather | solution.py:114
  40.3 3.3 fusion.106
  44.3 3.6 collective-permute-start
  47.9 3.2 fusion.107
  51.2 3.1 collective-permute-done
  54.3 10.8 %fusion.22 = (f32[1024,3]{0,1:T(4,128)S(1)}, f32[2048,1024,3]{1,0,2:T(8,128)}) fusion(pred[1024,2048]{0,1:T(8,128)(4,1)S(1)} %copy-done.4, bf16[1024,3,32]{0,2,1:T(8,128)(2,1)S(1)} %get-tuple-element.180, bf16[1024,3,32]{0,2,1:T(8,128)(2,1)S(1)} %get-tuple-element.179, bf16[1024,1,2,64]{0,3,2,1:T(8,128)(2,1)S(1)} %bitcast.303, ...), kind=kOutput, calls=%fused_computation.41 | convolution fusion | flops 825488384 | bytes 28192768 | tf_op jit(solution)/shard_map/qgrd,kgd->qgrk/dot_general | solution.py:64
  65.1 11.8 %fusion.24 = f32[1024,3]{0,1:T(4,128)S(1)} fusion(f32[2048,1024,3]{1,0,2:T(8,128)} %get-tuple-element.197, f32[1024,3]{0,1:T(4,128)S(1)} %get-tuple-element.185, pred[1024,2048]{0,1:T(8,128)(4,1)S(1)} %copy-done.4), kind=kLoop, calls=%fused_computation.43 | loop fusion | flops 31454208 | bytes 27287552 | tf_op jit(solution)/shard_map/reduce_sum | solution.py:72
  77.5 13.4 %fusion.55 = f32[1024,1,3,64]{0,3,2,1:T(8,128)} fusion(f32[2048,1024,3]{1,0,2:T(8,128)} %get-tuple-element.197, f32[1024,3]{0,1:T(4,128)S(1)} %get-tuple-element.185, pred[1024,2048]{0,1:T(8,128)(4,1)S(1)} %copy-done.4, f32[1024,3]{0,1:T(4,128)S(1)} %get-tuple-element.183, bf16[1024,1,2,64]{0,3,2,1:T(8,128)(2,1)S(1)} %maximum_convert_fusion, ...), kind=kOutput, calls=%fused_computation.70 | convolution fusion | flops 837484544 | bytes 28598272 | tf_op jit(solution)/shard_map/qgrk,kgd->qgrd/dot_general | solution.py:73
  91.5 264.8 %while.16 = (s32[]{:T(128)}, f32[1024,1,3]{0,2,1:T(4,128)S(1)}, f32[1024,1,3]{0,2,1:T(4,128)}, f32[1024,1,3,64]{0,3,2,1:T(8,128)}, s32[16]{0:T(128)}, /*index=5*...) while((s32[]{:T(128)}, f32[1024,1,3]{0,2,1:T(4,128)S(1)}, ...), condition=%wide.region_12.13_spmd, body=%wide.region_8.12_spmd.sunk | while | flops 424593408 | bytes 26533184 | solution.py:166
  94.1 1.9 compare_and_fusion.3
  99.2 2.5 fusion.120
  101.8 4.0 fusion.123
  110.7 1.9 compare_and_fusion.3
  115.8 2.5 fusion.120
  118.3 4.0 fusion.123
  127.2 1.9 compare_and_fusion.3
  132.3 2.5 fusion.120
  134.9 4.0 fusion.123
  143.8 1.9 compare_and_fusion.3
  148.9 2.5 fusion.120
  151.4 4.0 fusion.123
  165.4 2.5 fusion.120
  168.0 4.0 fusion.123
  182.0 2.5 fusion.120
  184.5 4.0 fusion.123
  198.5 2.5 fusion.120
  201.1 4.0 fusion.123
  215.1 2.5 fusion.120
  217.6 4.0 fusion.123
  231.6 2.5 fusion.120
  234.2 4.0 fusion.123
  248.2 2.5 fusion.120
  250.7 4.0 fusion.123
  259.6 1.9 compare_and_fusion.3
  264.7 2.5 fusion.120
  267.2 4.0 fusion.123
  281.3 2.5 fusion.120
  283.8 4.0 fusion.123
  297.8 2.5 fusion.120
  300.3 4.0 fusion.123
  314.4 2.5 fusion.120
  316.9 4.0 fusion.123
  330.9 2.5 fusion.120
  333.4 4.0 fusion.123
  347.4 2.5 fusion.120
  350.0 4.0 fusion.123
  357.5 3.8 convolution_convert_fusion
  365.2 17.5 %reduce-window.19 = s32[32,8,128]{2,1,0:T(8,128)} reduce-window(s32[32,8,128]{2,1,0:T(8,128)} %fusion.88, s32[]{:T(128)} %constant.122.clone.1), window={size=1x1x128 pad=0_0x0_0x127_0}, to_apply=%region_14.15 | reduce-window | flops 4161536 | bytes 262148 | tf_op jit(solution)/shard_map/reduce-window.2
  393.9 4.5 scatter_custom_fusion.1
  398.4 4.9 scatter_custom_fusion
  407.2 10.7 %gather_fusion = bf16[2048,1536]{1,0:T(8,128)(2,1)} fusion(bf16[128,1536]{1,0:T(8,128)(2,1)S(1)} %multiply_convert_fusion, s32[2048]{0:T(1024)} %fusion.89), kind=kCustom, calls=%fused_computation | custom fusion | bytes 12591104 | tf_op jit(solution)/shard_map/gather | solution.py:189
  417.8 3.3 broadcast_select_fusion
  421.2 80.2 %all_to_all.10 = bf16[16,2,64,1536]{3,2,1,0:T(8,128)(2,1)S(1)} all-to-all(bf16[16,2,64,1536]{3,2,1,0:T(8,128)(2,1)S(1)} %broadcast_select_fusion), channel_id=1, replica_groups=mesh['tok'=16,'head'=8] {'tok'}, dimensions={0} | all-to-all | bytes 12582912 | tf_op jit(solution)/shard_map/all_to_all | solution.py:191
  501.4 2.7 copy-done.6
  504.1 4.9 fusion.29
  509.0 11.9 %convert_bitcast_fusion = bf16[16,2,64,1536]{3,2,0,1:T(8,128)(2,1)} fusion(bf16[2,512,1536]{2,1,0:T(8,128)(2,1)S(1)} %copy-done, f32[2,16,64,512]{3,2,1,0:T(8,128)} %fusion.29, bf16[2,1536,512]{2,1,0:T(8,128)(2,1)} %param.31, bf16[16,2,64,1536]{3,2,1,0:T(8,128)(2,1)} %copy-done.6), kind=kOutput, calls=%fused_computation.50 | convolution fusion | flops 6451888128 | bytes 23068672 | tf_op jit(solution)/shard_map/secf,efd->secd/dot_general | solution.py:195
  520.9 6.1 copy.77
  527.0 6.6 all-to-all-start.1
  533.6 98.2 %all-to-all-done.1 = bf16[16,2,64,1536]{3,2,1,0:T(8,128)(2,1)} async-done(((bf16[16,2,64,1536]{3,2,1,0:T(8,128)(2,1)}), bf16[16,2,64,1536]{3,2,1,0:T(8,128)(2,1)}, u32[]{:S(2)}, u32[]{:S(2)}) %all-to-all-start.1) | async-done | bytes 6291488 | tf_op jit(solution)/shard_map/all_to_all | solution.py:198
  631.8 10.9 %gather_fusion.1 = bf16[1024,1536]{1,0:T(8,128)(2,1)} fusion(bf16[2048,1536]{1,0:T(8,128)(2,1)} %bitcast.55, s32[1024]{0:T(1024)S(1)} %broadcast_clamp_fusion), kind=kCustom, calls=%fused_computation.1 | custom fusion | bytes 6295552 | tf_op jit(solution)/shard_map/gather | solution.py:201
  642.8 14.7 %fusion.105 = (bf16[128,1,1536]{2,1,0:T(2,128)(2,1)S(1)}, bf16[128,1,1536]{2,1,0:T(2,128)(2,1)S(1)}, bf16[128,1,1536]{2,1,0:T(2,128)(2,1)S(1)}, bf16[128,1,1536]...) fusion(bf16[128,8,1536]{2,1,0:T(8,128)(2,1)} %bitcast.281), kind=kLoop, calls=%fused_computation.191 | loop fusion | bytes 6291456 | tf_op jit(solution)/shard_map/slice | solution.py:204
  (385 shorter events, 171.5 us)
Async XLA Ops:
  6.5 502.4 %copy-start = (bf16[2,512,1536]{2,1,0:T(8,128)(2,1)S(1)}, bf16[2,512,1536]{2,1,0:T(8,128)(2,1)}, u32[]{:S(2)}) copy-start(bf16[2,512,1536]{2,1,0:T(8,128)(2,1)} %param.33) | copy-start | bytes 9437188
  6.5 33.8 %all-gather.3.cloned.1.call-start = ((), (), s32[]{:S(2)}) async-start(), calls=%async_computation.3 | async-start | bytes 3538944 | tf_op jit(solution)/shard_map/all_gather | solution.py:114
  9.8 81.2 %all-gather.5.cloned.1.call-start = ((), (), s32[]{:S(2)}) async-start(), calls=%async_computation.4 | async-start | bytes 2228224 | tf_op jit(solution)/shard_map/all_gather | solution.py:159
  10.5 394.1 %reduce-scatter.2.cloned.1.call-start = ((), (), s32[]{:S(2)}) async-start(), calls=%async_computation.5 | async-start | bytes 3538944 | tf_op jit(solution)/shard_map/reduce_scatter | solution.py:172
  40.3 14.0 %copy-start.4 = (pred[1024,2048]{0,1:T(8,128)(4,1)S(1)}, pred[1024,2048]{0,1:T(8,128)(4,1)}, u32[]{:S(2)}) copy-start(pred[1024,2048]{0,1:T(8,128)(4,1)} %compare_and_fusion.1) | copy-start | bytes 6291460
  44.3 10.0 %collective-permute-start = (bf16[1024,128]{0,1:T(8,128)(2,1)S(1)}, bf16[1024,128]{0,1:T(8,128)(2,1)S(1)}, u32[]{:S(2)}, u32[]{:S(2)}) collective-permute-start(bf16[1024,128]{0,1:T(8,128)(2,1)S(1)} %bitcast.295), channel_id=1, source_target_pairs={{0,8},{8,16},{16,24},{24,32},{32,40},{40,48},{48,56},{56,64},{64,7... | collective-permute-start | bytes 786440 | tf_op jit(solution)/shard_map/ppermute | solution.py:21
  99.2 2.5 copy-start.1
  99.2 2.5 copy-start.5
  105.8 1.6 copy-start.8
  115.8 2.5 copy-start.1
  115.8 2.5 copy-start.5
  122.4 1.6 copy-start.8
  132.3 2.5 copy-start.1
  132.3 2.5 copy-start.5
  138.9 1.6 copy-start.8
  148.9 2.5 copy-start.1
  148.9 2.5 copy-start.5
  155.5 1.6 copy-start.8
  165.4 2.5 copy-start.1
  165.4 2.5 copy-start.5
  172.0 1.6 copy-start.8
  182.0 2.5 copy-start.1
  182.0 2.5 copy-start.5
  188.6 1.6 copy-start.8
  198.5 2.5 copy-start.1
  198.5 2.5 copy-start.5
  205.1 1.6 copy-start.8
  215.1 2.5 copy-start.1
  215.1 2.5 copy-start.5
  221.7 1.6 copy-start.8
  231.6 2.5 copy-start.1
  231.6 2.5 copy-start.5
  238.2 1.6 copy-start.8
  248.2 2.5 copy-start.1
  248.2 2.5 copy-start.5
  254.7 1.6 copy-start.8
  264.7 2.5 copy-start.1
  264.7 2.5 copy-start.5
  271.3 1.6 copy-start.8
  281.3 2.5 copy-start.1
  281.3 2.5 copy-start.5
  287.8 1.6 copy-start.8
  297.8 2.5 copy-start.1
  297.8 2.5 copy-start.5
  304.4 1.6 copy-start.8
  314.3 2.5 copy-start.1
  314.3 2.5 copy-start.5
  320.9 1.6 copy-start.8
  330.9 2.5 copy-start.1
  330.9 2.5 copy-start.5
  337.5 1.6 copy-start.8
  347.4 2.5 copy-start.1
  347.4 2.5 copy-start.5
  354.0 1.6 copy-start.8
  356.3 5.0 copy-start.10
  356.3 48.4 %copy-start.2 = (bf16[128,1536]{1,0:T(8,128)(2,1)S(1)}, bf16[128,1536]{1,0:T(8,128)(2,1)}, u32[]{:S(2)}) copy-start(bf16[128,1536]{1,0:T(8,128)(2,1)} %param.18) | copy-start | bytes 1179652
  393.9 4.5 copy-start.11
  421.2 82.9 %copy-start.14 = (bf16[2,1536,512]{2,1,0:T(8,128)(2,1)S(1)}, bf16[2,1536,512]{2,1,0:T(8,128)(2,1)}, u32[]{:S(2)}) copy-start(bf16[2,1536,512]{2,1,0:T(8,128)(2,1)} %param.32) | copy-start | bytes 9437188
  501.4 2.7 copy-start.6
  527.0 6.6 copy-start.12
  527.0 6.6 copy-start.13
  527.0 104.8 %all-to-all-start.1 = ((bf16[16,2,64,1536]{3,2,1,0:T(8,128)(2,1)}), bf16[16,2,64,1536]{3,2,1,0:T(8,128)(2,1)}, u32[]{:S(2)}, u32[]{:S(2)}) async-start(bf16[16,2,64,1536]{3,2,1,0:T(8,128)(2,1)} %copy.77), calls=%async_computation.2 | async-start | bytes 12582912 | tf_op jit(solution)/shard_map/all_to_all | solution.py:198
  642.8 14.7 %copy-start.3 = (bf16[128,1536]{1,0:T(8,128)(2,1)S(1)}, bf16[128,1536]{1,0:T(8,128)(2,1)}, u32[]{:S(2)}) copy-start(bf16[128,1536]{1,0:T(8,128)(2,1)} %param.18) | copy-start | bytes 1179652
  642.8 14.7 %copy-start.7 = (bf16[128,1536]{1,0:T(8,128)(2,1)S(1)}, bf16[128,1536]{1,0:T(8,128)(2,1)}, u32[]{:S(2)}) copy-start(bf16[128,1536]{1,0:T(8,128)(2,1)} %reduce-scatter.2.cloned.1.call-done) | copy-start | bytes 1179652
  (16 other events, 9.6 us)
Sparse Core Ops, SparseCore 0:
  9.9 30.3 all-gather.2
  42.5 44.5 all-gather.4
  361.4 36.3 reduce-scatter.1
where the time goes:
time: 673 us; the launch traced here: 666 us
  matrix products  156 us (23%)
  local copies, waits for them, and re-layouts  148 us (22%)
  other arithmetic  130 us (19%)
  waiting for transfers between devices  116 us (17%)
  blocking collectives  80.2 us (12%)
  between operations  13.4 us (2%)
  loops' own time  11.4 us (2%)
  starting transfers between devices  10.2 us (2%)
    all_to_all x1, waiting for transfers between devices, local(): lax.all_to_all(answered, 'tok', split_axis=0, concat_axis=0, tiled=True)  98.2 us
    all_to_all x1, blocking collectives, local(): lax.all_to_all(outgoing, 'tok', split_axis=0, concat_axis=0, tiled=True)  80.2 us
    dot_general x17, matrix products, absorb(): jnp.einsum('qgrk,kgd->qgrd', weights.astype(jnp.bfloat16), value_rows, pr...  78.2 us
    dynamic_slice x48, local copies, waits for them, and re-layouts, local(): lax.scan(advance, state, (stacked, jnp.arange(length_rows // key_block, d...  70.7 us
    dot_general x17, matrix products, absorb(): jnp.einsum('qgrd,kgd->qgrk', query_heads, key_rows, preferred_element_typ...  50.7 us
    reduce_sum x17, other arithmetic, absorb(): weight_sum = weight_sum * factor + jnp.sum(weights, axis=-1)  37.1 us
    and x16, other arithmetic, one_block(): (slab_of[None, :] == row_slab[:, None]) & (inside < limit_rows)[None, :]  30 us
    reduce_sum x19, other arithmetic, lookup(): return jnp.sum(jnp.where(index[..., None] == entries, table, 0), axis=-1)  19.8 us
  transfers between devices with their start and end apart: 5, of which 3 were waited for; matrix products, arithmetic and copies ran while one was open for 15% of the time, Pallas kernels for 0%

commit v1 on v0

v1 whole, which is shorter than its diff:
```python
import functools

import jax
import jax.numpy as jnp
from jax import lax
from jax.experimental import pallas as pl
from jax.experimental.pallas import tpu as pltpu
from jax.sharding import PartitionSpec as P

HS = 64
EXPERTS = 32
TOPK = 8
PREFIX = 512
NEG_FILL = -1e30
NORM_EPS = 1e-06
LOG2E = 1.4426950408889634
BF = jnp.bfloat16
F32 = jnp.float32
VMEM_CAP = 60 * 1024 * 1024


def rms_scale(values, gain):
    widened = values.astype(F32)
    spread = jnp.mean(widened * widened, axis=-1, keepdims=True)
    return widened * lax.rsqrt(spread + NORM_EPS) * gain


def request_tables(window, own, group_ids, prefix_owner, slab_fill):
    reqs = group_ids.shape[0]
    ids = jnp.arange(reqs, dtype=jnp.int32)
    slabs = jnp.arange(prefix_owner.shape[0], dtype=jnp.int32)
    begins = jnp.sum((window[None, :] < ids[:, None]).astype(jnp.int32), axis=1)
    slab_of = jnp.sum(jnp.where(group_ids[:, None] == slabs, prefix_owner, 0), axis=1)
    fill_of = jnp.sum(jnp.where(slab_of[:, None] == slabs, slab_fill, 0), axis=1)
    packed = (begins * 16 + slab_of) * 1024 + fill_of
    mine = jnp.sum(jnp.where(own[None, :] == ids[:, None], packed[:, None], 0), axis=0)
    return mine // (16 * 1024), (mine // 1024) % 16, mine % 1024


def project_kernel(x_ref, wq_ref, wkv_ref, cos_ref, sin_ref, q_ref, kv_ref):
    x = x_ref[...]
    heads = wq_ref.shape[1] // HS
    pq = jnp.dot(x, wq_ref[...], preferred_element_type=F32)
    pkv = jnp.dot(x, wkv_ref[...], preferred_element_type=F32)
    both = jnp.concatenate([pq, pkv], axis=1)
    width = both.shape[1]
    lane = lax.broadcasted_iota(jnp.int32, both.shape, 1)
    swapped = jnp.where(
        lane % HS < HS // 2,
        pltpu.roll(both, width - HS // 2, 1),
        pltpu.roll(both, HS // 2, 1),
    )
    copies = -(-width // 128)
    cos = jnp.concatenate([cos_ref[...]] * copies, axis=1)[:, :width]
    sin = jnp.concatenate([sin_ref[...]] * copies, axis=1)[:, :width]
    turned = jnp.where(lane < (heads + 1) * HS, both * cos + swapped * sin, both).astype(BF)
    pad = jnp.zeros((x.shape[0], HS), BF)
    for head in range(heads):
        q_ref[head] = jnp.concatenate([turned[:, head * HS : (head + 1) * HS], pad], axis=1)
    kv_ref[...] = turned[:, heads * HS :]


def project(x, w_query, w_keyval, cos, sin, rows=256):
    length = x.shape[0]
    heads = w_query.shape[1] // HS
    whole = lambda a: pl.BlockSpec(a.shape, lambda i: (0,) * a.ndim)
    return pl.pallas_call(
        project_kernel,
        grid=(length // rows,),
        in_specs=[
            pl.BlockSpec((rows, x.shape[1]), lambda i: (i, 0)),
            whole(w_query),
            whole(w_keyval),
            pl.BlockSpec((rows, 128), lambda i: (i, 0)),
            pl.BlockSpec((rows, 128), lambda i: (i, 0)),
        ],
        out_specs=[
            pl.BlockSpec((heads, rows, 128), lambda i: (0, i, 0)),
            pl.BlockSpec((rows, 128), lambda i: (i, 0)),
        ],
        out_shape=[
            jax.ShapeDtypeStruct((heads, length, 128), BF),
            jax.ShapeDtypeStruct((length, 128), BF),
        ],
        compiler_params=pltpu.CompilerParams(vmem_limit_bytes=VMEM_CAP),
        name="project",
    )(x, w_query, w_keyval, cos, sin)


def attend_kernel(
    steps_ref, used_ref, fill_ref, q_ref, prev_ref, now_ref, cache_ref, rows_ref, wout_ref, out_ref, near_ref
):
    block = pl.program_id(0)
    heads, span = q_ref.shape[0], q_ref.shape[1]
    row_len = now_ref.shape[0]
    scale = HS ** (-0.5) * LOG2E

    @pl.when(block == 0)
    def _():
        near_ref[:row_len] = prev_ref[...]
        near_ref[row_len:] = now_ref[...]

    queries = jnp.concatenate([q_ref[h] for h in range(heads)], axis=0)
    begins = jnp.concatenate([rows_ref[0:1]] * heads, axis=1)
    slabs = jnp.concatenate([rows_ref[1:2]] * heads, axis=1)
    offset = row_len + block * span
    wide = heads * span

    def scores(kv):
        return lax.dot_general(kv, queries, (((1,), (1,)), ((), ())), preferred_element_type=F32)

    def absorb(s, kv, carry):
        peak, total, acc = carry
        peak_new = jnp.maximum(peak, jnp.max(s, axis=0, keepdims=True))
        factor = jnp.exp2((peak - peak_new) * scale)
        weights = jnp.exp2((s - peak_new) * scale)
        total = total * factor + jnp.sum(weights, axis=0, keepdims=True)
        values = kv.T[HS:]
        acc = acc * factor + jnp.dot(values, weights.astype(BF), preferred_element_type=F32)
        return peak_new, total, acc

    kv = near_ref[pl.ds(pl.multiple_of(offset, span), span)]
    key = lax.broadcasted_iota(jnp.int32, (span, wide), 0)
    query = lax.broadcasted_iota(jnp.int32, (span, wide), 1) % span
    s = jnp.where((key <= query) & (key >= begins - offset), scores(kv), NEG_FILL)
    carry = (
        jnp.full((1, wide), NEG_FILL, F32),
        jnp.zeros((1, wide), F32),
        jnp.zeros((HS, wide), F32),
    )
    carry = absorb(s, kv, carry)

    chunk = 2 * span

    def near_step(step, carry):
        first = pl.multiple_of(offset - (step + 1) * chunk, span)
        kv = near_ref[pl.ds(first, chunk)]
        key = lax.broadcasted_iota(jnp.int32, (chunk, wide), 0)
        s = jnp.where(key >= begins - first, scores(kv), NEG_FILL)
        return absorb(s, kv, carry)

    carry = lax.fori_loop(0, steps_ref[block], near_step, carry)

    def far_step(step, carry):
        slab = used_ref[block, step + 1]
        kv = cache_ref[pl.ds(pl.multiple_of(slab * PREFIX, PREFIX), PREFIX)]
        key = lax.broadcasted_iota(jnp.int32, (PREFIX, wide), 0)
        limit = jnp.where(slabs == slab, fill_ref[slab], 0)
        s = jnp.where(key < limit, scores(kv), NEG_FILL)
        return absorb(s, kv, carry)

    _, total, acc = lax.fori_loop(0, used_ref[block, 0], far_step, carry)
    mixed = (acc / total).T
    mixed = jnp.concatenate([mixed[h * span : (h + 1) * span] for h in range(heads)], axis=1)
    out_ref[...] = jnp.dot(mixed.astype(BF), wout_ref[...], preferred_element_type=F32).astype(BF)


def attend(q, kv_prev, kv_now, cache, rows, steps, used, fill, w_out, span=128):
    heads, length, _ = q.shape
    whole = lambda a: pl.BlockSpec(a.shape, lambda i, *_: (0,) * a.ndim)
    return pl.pallas_call(
        attend_kernel,
        grid_spec=pltpu.PrefetchScalarGridSpec(
            num_scalar_prefetch=3,
            grid=(length // span,),
            in_specs=[
                pl.BlockSpec((heads, span, 128), lambda i, *_: (0, i, 0)),
                whole(kv_prev),
                whole(kv_now),
                whole(cache),
                pl.BlockSpec((8, span), lambda i, *_: (0, i)),
                whole(w_out),
            ],
            out_specs=pl.BlockSpec((span, w_out.shape[1]), lambda i, *_: (i, 0)),
            scratch_shapes=[pltpu.VMEM((2 * length, 128), BF)],
        ),
        out_shape=jax.ShapeDtypeStruct((length, w_out.shape[1]), BF),
        compiler_params=pltpu.CompilerParams(vmem_limit_bytes=VMEM_CAP),
        name="attend",
    )(steps, used, fill, q, kv_prev, kv_now, cache, rows, w_out)


def expert_kernel(first_ref, x_ref, gates_ref, wg_ref, wu_ref, wd_ref, out_ref):
    x = x_ref[...]
    gates = gates_ref[...]
    lane = lax.broadcasted_iota(jnp.int32, gates.shape, 1)
    total = jnp.zeros((x.shape[0], wd_ref.shape[2]), F32)
    for e in range(wg_ref.shape[0]):
        gate = jnp.sum(jnp.where(lane == first_ref[0] + e, gates, 0.0), axis=1, keepdims=True)
        g = jnp.dot(x, wg_ref[e], preferred_element_type=F32)
        u = jnp.dot(x, wu_ref[e], preferred_element_type=F32)
        act = (g / (1.0 + jnp.exp(-g)) * u).astype(BF)
        o = jnp.dot(act, wd_ref[e], preferred_element_type=F32).astype(BF).astype(F32)
        total = total + gate * o
    out_ref[...] = total.astype(BF)


def run_experts(first, x, gates, w_gate, w_up, w_down, rows=256):
    length, width = x.shape
    whole = lambda a: pl.BlockSpec(a.shape, lambda i, *_: (0,) * a.ndim, pipeline_mode=pl.Buffered(1))
    return pl.pallas_call(
        expert_kernel,
        grid_spec=pltpu.PrefetchScalarGridSpec(
            num_scalar_prefetch=1,
            grid=(length // rows,),
            in_specs=[
                pl.BlockSpec((rows, width), lambda i, *_: (i, 0)),
                pl.BlockSpec((rows, gates.shape[1]), lambda i, *_: (i, 0)),
                whole(w_gate),
                whole(w_up),
                whole(w_down),
            ],
            out_specs=pl.BlockSpec((rows, width), lambda i, *_: (i, 0)),
        ),
        out_shape=jax.ShapeDtypeStruct((length, width), BF),
        compiler_params=pltpu.CompilerParams(vmem_limit_bytes=VMEM_CAP),
        name="experts",
    )(first, x, gates, w_gate, w_up, w_down)


def local(
    tokens,
    segments,
    group_ids,
    prefix_owner,
    slab_fill,
    prefix_cache,
    attn_gain,
    w_query,
    w_keyval,
    w_out,
    ffn_gain,
    routes,
    route_gates,
    w_gate,
    w_up,
    w_down,
):
    tok_count = lax.axis_size("tok")
    head_count = lax.axis_size("head")
    place = lax.axis_index("tok")
    row_len = tokens.shape[0] * head_count
    normed = rms_scale(tokens, attn_gain).astype(BF)
    gathered = lax.all_gather(normed, "head", axis=0, tiled=True)
    cache = lax.all_gather(prefix_cache, "tok", axis=0, tiled=True)

    padded = jnp.concatenate([jnp.full((row_len,), -1, jnp.int32), segments])
    window = lax.dynamic_slice_in_dim(padded, place * row_len, 2 * row_len, 0)
    own = window[row_len:]
    begins, slabs, fills = request_tables(window, own, group_ids, prefix_owner, slab_fill)
    positions = fills + row_len + jnp.arange(row_len, dtype=jnp.int32) - begins
    lane = jnp.arange(128, dtype=jnp.int32)
    steps_idx = (lane % (HS // 2)).astype(F32)
    inverse = jnp.exp(steps_idx * (-2.0 * jnp.log(10000.0) / HS))
    angles = positions.astype(F32)[:, None] * inverse[None, :]
    cos = jnp.cos(angles)
    sin = jnp.where(lane % HS < HS // 2, -jnp.sin(angles), jnp.sin(angles))

    span = 128
    blocks = row_len // span
    first_begin = begins.reshape(blocks, span)[:, 0]
    ends = row_len + jnp.arange(blocks, dtype=jnp.int32) * span
    steps = jnp.maximum(ends - first_begin + 2 * span - 1, 0) // (2 * span)
    ids = jnp.arange(tok_count, dtype=jnp.int32)
    present = jnp.max((slabs.reshape(blocks, span)[:, :, None] == ids).astype(jnp.int32), axis=1)
    earlier = jnp.sum(jnp.where(ids[:, None] < ids[None, :], present[:, :, None], 0), axis=1)
    listed = (present[:, None, :] == 1) & (earlier[:, None, :] == ids[None, :, None])
    used = jnp.sum(jnp.where(listed, ids, 0), axis=2)
    used = jnp.concatenate([jnp.sum(present, axis=1, keepdims=True), used], axis=1)
    rows = jnp.concatenate([begins[None], slabs[None], jnp.zeros((6, row_len), jnp.int32)], axis=0)

    q, kv_now = project(gathered, w_query, w_keyval, cos, sin)
    kv_prev = lax.ppermute(kv_now, "tok", [(i, i + 1) for i in range(tok_count - 1)])
    partial = attend(q, kv_prev, kv_now, cache, rows, steps, used, slab_fill, w_out)
    attended = lax.psum_scatter(partial, "head", scatter_dimension=0, tiled=True).astype(F32)
    hidden = tokens.astype(F32) + attended
    expert_in = rms_scale(hidden, ffn_gain).astype(BF)

    experts = jnp.arange(EXPERTS, dtype=jnp.int32)
    gates = jnp.sum(jnp.where(routes[:, :, None] == experts, route_gates[:, :, None], 0.0), axis=1)
    gates_all = lax.all_gather(gates, "tok", axis=0, tiled=True)
    arrived = lax.all_gather(expert_in, "tok", axis=0, tiled=True)
    first = (place * w_gate.shape[0]).astype(jnp.int32).reshape(1)
    answered = run_experts(first, arrived, gates_all, w_gate, w_up, w_down)
    mixture = lax.psum_scatter(answered, "tok", scatter_dimension=0, tiled=True)
    return (hidden + mixture.astype(F32)).astype(BF)


def solution(mesh):
    return jax.shard_map(
        local,
        mesh=mesh,
        in_specs=(
            P(("tok", "head"), None),
            P(),
            P(),
            P(),
            P(),
            P("tok", "head"),
            P(),
            P(None, "head"),
            P(None, "head"),
            P("head", None),
            P(),
            P(("tok", "head"), None),
            P(("tok", "head"), None),
            P("tok", None, None),
            P("tok", None, None),
            P("tok", None, None),
        ),
        out_specs=P(("tok", "head"), None),
        check_vma=False,
    )
```

time: 673 us -> 332 us (0.49); the launches traced: 666 us -> 331 us
  matrix products: 156 us -> 0 us
  local copies, waits for them, and re-layouts: 148 us -> 4.73 us
  other arithmetic: 130 us -> 15.7 us
  waiting for transfers between devices: 116 us -> 207 us
  Pallas kernels: 0 us -> 58.2 us
  blocking collectives: 80.2 us -> 28.5 us
  loops' own time: 11.4 us -> 0 us
    dot_general x39 -> x0, matrix products: 156 us -> none  [the longest x17 78.2 us: absorb(): jnp.einsum('qgrk,kgd->qgrd', weights.astype(jnp.bfloat16), value_rows, pr...]
    reduce_scatter x1 -> x2, waiting for transfers between devices: 0.01 us -> 118 us  [the longest x1 81.4 us: local(): mixture = lax.psum_scatter(answered, 'tok', scatter_dimension=0, tiled=True)]
    all_to_all x1 -> x0, waiting for transfers between devices: 98.2 us -> none  [local(): lax.all_to_all(answered, 'tok', split_axis=0, concat_axis=0, tiled=True)]
    all_to_all x1 -> x0, blocking collectives: 80.2 us -> none  [local(): lax.all_to_all(outgoing, 'tok', split_axis=0, concat_axis=0, tiled=True)]
    all_gather x2 -> x3, waiting for transfers between devices: 14.1 us -> 88.9 us  [the longest x1 36.6 us: local(): cache = lax.all_gather(prefix_cache, 'tok', axis=0, tiled=True)]
    dynamic_slice x50 -> x1, local copies, waits for them, and re-layouts: 72 us -> 0.69 us  [local(): window = lax.dynamic_slice_in_dim(padded, place * row_len, 2 * row_len, 0)]
    pallas_call x0 -> x3, Pallas kernels: none -> 58.2 us  [the longest x1 27.6 us: run_experts(): pl.pallas_call(expert_kernel, grid_spec=pltpu.PrefetchScalarGridSpec(num_...]
    reduce_sum x37 -> x8, other arithmetic: 57.6 us -> 2.28 us  [the longest x1 0.76 us: request_tables(): jnp.sum(jnp.where(group_ids[:, None] == slabs, prefix_owner, 0), axis=1)]
  transfers between devices with their start and end apart: 5 -> 6, of which waited for: 3 -> 5; matrix products, arithmetic and copies ran while one was open for 15% -> 4% of each run, Pallas kernels for 0% -> 2%
where the time goes in v1:
time: 332 us; the launch traced here: 331 us
  waiting for transfers between devices  207 us (62%)
  Pallas kernels  58.2 us (18%)
  blocking collectives  28.5 us (9%)
  other arithmetic  15.7 us (5%)
  between operations  13.3 us (4%)
  local copies, waits for them, and re-layouts  4.73 us (1%)
  starting transfers between devices  3.56 us (1%)
    reduce_scatter x1, waiting for transfers between devices, local(): mixture = lax.psum_scatter(answered, 'tok', scatter_dimension=0, tiled=True)  81.4 us
    all_gather x1, waiting for transfers between devices, local(): cache = lax.all_gather(prefix_cache, 'tok', axis=0, tiled=True)  36.6 us
    reduce_scatter x1, waiting for transfers between devices, local(): lax.psum_scatter(partial, 'head', scatter_dimension=0, tiled=True)  36.4 us
    all_gather x1, waiting for transfers between devices, local(): arrived = lax.all_gather(expert_in, 'tok', axis=0, tiled=True)  32.7 us
    all_gather x1, blocking collectives, local(): gates_all = lax.all_gather(gates, 'tok', axis=0, tiled=True)  28.5 us
    pallas_call x1, Pallas kernels, run_experts(): pl.pallas_call(expert_kernel, grid_spec=pltpu.PrefetchScalarGridSpec(num_...  27.6 us
    pallas_call x1, Pallas kernels, attend(): pl.pallas_call(attend_kernel, grid_spec=pltpu.PrefetchScalarGridSpec(num_...  23.9 us
    all_gather x1, waiting for transfers between devices, local(): gathered = lax.all_gather(normed, 'head', axis=0, tiled=True)  19.6 us
  transfers between devices with their start and end apart: 6, of which 5 were waited for; matrix products, arithmetic and copies ran while one was open for 4% of the time, Pallas kernels for 2%

profile of v1, /device:TPU:0, one launch (start us, length us, event | category | flops | bytes accessed | tf_op | source)
XLA Modules:
  0.0 331.4 jit_solution(18071001410971440409)
XLA Ops:
  6.5 0.0 all-gather.4.cloned.1.call-start
  6.5 1.2 fusion
  7.7 1.9 fusion.2
  9.6 0.0 all-gather.4.cloned.1.call-update
  9.6 0.0 all-gather.6.cloned.1.call-start
  9.7 0.7 all-gather.6.cloned.1.call-update
  10.4 0.0 reduce-scatter.3.cloned.1.call-start
  10.4 0.7 pad_dynamic-slice_fusion
  11.1 0.7 pad_dynamic-slice_fusion.1
  11.8 0.8 select_reduce_fusion.5
  12.6 0.7 select_reduce_fusion.4
  13.3 0.2 convert_reduce_fusion
  13.5 0.1 select_reduce_fusion
  13.7 0.2 convert_reduce_fusion.1
  13.9 0.1 reduce_sum.99
  14.0 0.1 copy.30
  14.1 2.2 copy.31.wq_ref
  16.4 0.1 slice_reduce_fusion
  16.5 0.1 select_reduce_fusion.3
  16.6 0.2 select_reduce_fusion.2
  16.8 0.6 and_select_fusion.5.steps_ref
  17.4 0.1 and_select_fusion.2
  17.5 3.1 negate_select_fusion
  20.6 19.6 %all-gather.4.cloned.1.call-done.x_ref = bf16[1024,1536]{1,0:T(8,128)(2,1)} async-done(((bf16[128,1536]{1,0:T(8,128)(2,1)}), bf16[1024,1536]{1,0:T(8,128)(2,1)}) %all-gather.4.cloned.1.call-update) | async-done | bytes 3145744 | tf_op jit(solution)/shard_map/all_gather | solution.py:244
  40.2 6.6 %project.1 = (bf16[3,1024,128]{2,1,0:T(8,128)(2,1)}, bf16[1024,128]{1,0:T(8,128)(2,1)}) custom-call(bf16[1024,1536]{1,0:T(8,128)(2,1)} %all-gather.4.cloned.1.call-done.x_ref, bf16[1536,192]{1,0:T(8,128)(2,1)} %copy.31.wq_ref, bf16[1536,128]{1,0:T(8,128)(2,1)} %wkv_ref.1, f32[1024,128]{1,0:T(8,128)} %get-tuple-element.10.cos_ref, ...), custom_call_target="tpu_custom_call" | custom-call | tf_op jit(solution)/shard_map/project/pallas_call | solution.py:67
  46.8 3.4 %collective-permute-start = (bf16[1024,128]{1,0:T(8,128)(2,1)}, bf16[1024,128]{1,0:T(8,128)(2,1)S(1)}, u32[]{:S(2)}, u32[]{:S(2)}) collective-permute-start(bf16[1024,128]{1,0:T(8,128)(2,1)} %get-tuple-element.8.now_ref), channel_id=1, source_target_pairs={{0,8},{8,16},{16,24},{24,32},{32,40},{40,48},{48,56},{56,64},{64,7... | collective-permute-start | bytes 786440 | tf_op jit(solution)/shard_map/ppermute | solution.py:273
  50.2 0.7 pad_add_fusion.used_ref
  50.9 0.1 pad.3.clone
  50.9 0.7 add_add_fusion.rows_ref
  51.6 36.6 %all-gather.6.cloned.1.call-done.cache_ref = bf16[8192,128]{1,0:T(8,128)(2,1)} async-done(((bf16[512,128]{1,0:T(8,128)(2,1)}), bf16[8192,128]{1,0:T(8,128)(2,1)}) %all-gather.6.cloned.1.call-update) | async-done | bytes 2097168 | tf_op jit(solution)/shard_map/all_gather | solution.py:245
  88.2 0.0 collective-permute-done.prev_ref
  88.2 0.0 copy-start.2
  88.2 0.7 copy-done.2
  88.9 23.9 %attend.1 = bf16[1024,1536]{1,0:T(8,128)(2,1)} custom-call(s32[8]{0:T(128)} %and_select_fusion.5.steps_ref, s32[8,17]{1,0:T(8,128)} %pad_add_fusion.used_ref, s32[16]{0:T(128)} %fill_ref.1, bf16[3,1024,128]{2,1,0:T(8,128)(2,1)} %get-tuple-element.7.q_ref, bf16[1024,128]{1,0:T(8,128)(2,1)} %copy-done.2, bf16[1024,128]{1,0:T(8,128)(2,1)} %get-tuple-element.8.now_ref, ...), custom_call_target="tpu_custom_call" | custom-call | tf_op jit(solution)/shard_map/attend/pallas_call | solution.py:161
  112.8 0.0 copy-start
  112.8 0.0 copy-start.3
  112.9 0.0 copy-start.4
  112.9 0.0 copy-start.5
  112.9 0.0 reduce-scatter.3.cloned.1.call-update
  112.9 0.0 all-gather.8.cloned.1.call-start
  113.0 36.4 %reduce-scatter.3.cloned.1.call-done = bf16[128,1536]{1,0:T(8,128)(2,1)} async-done(((bf16[1024,1536]{1,0:T(8,128)(2,1)}), bf16[128,1536]{1,0:T(8,128)(2,1)}) %reduce-scatter.3.cloned.1.call-update) | async-done | bytes 393232 | tf_op jit(solution)/shard_map/reduce_scatter | solution.py:275
  149.4 0.0 copy-done
  149.4 1.2 multiply_reduce_fusion
  150.6 0.0 copy-done.3
  150.6 1.9 multiply_convert_fusion
  152.5 0.0 all-gather.8.cloned.1.call-update
  152.5 0.0 reduce-scatter.5.cloned.1.call-start
  152.6 0.0 copy-done.4
  152.6 0.0 copy-done.5
  152.6 0.1 copy.32
  152.7 28.5 %all_gather.15.gates_ref = f32[2048,32]{1,0:T(8,128)} all-gather(f32[128,32]{1,0:T(8,128)S(1)} %copy.32), channel_id=1, replica_groups=mesh['tok'=16,'head'=8] {'tok'}, dimensions={0}, use_global_device_ids=true | all-gather | bytes 278528 | tf_op jit(solution)/shard_map/all_gather | solution.py:281
  181.2 32.7 %all-gather.8.cloned.1.call-done.x_ref = bf16[2048,1536]{1,0:T(8,128)(2,1)} async-done(((bf16[128,1536]{1,0:T(8,128)(2,1)}), bf16[2048,1536]{1,0:T(8,128)(2,1)}) %all-gather.8.cloned.1.call-update) | async-done | bytes 6291472 | tf_op jit(solution)/shard_map/all_gather | solution.py:282
  213.9 27.6 %experts.1 = bf16[2048,1536]{1,0:T(8,128)(2,1)} custom-call(s32[1]{0:T(128)} %bitcast.3.first_ref, bf16[2048,1536]{1,0:T(8,128)(2,1)} %all-gather.8.cloned.1.call-done.x_ref, f32[2048,32]{1,0:T(8,128)} %all_gather.15.gates_ref, bf16[2,1536,512]{2,1,0:T(8,128)(2,1)} %wg_ref.1, bf16[2,1536,512]{2,1,0:T(8,128)(2,1)} %wu_ref.1, bf16[2,512,1536]{2,1,0:T(8,128)(2,1)} %wd_ref.1), custom_call_target="tpu_custom_call" | custom-call | tf_op jit(solution)/shard_map/experts/pallas_call | solution.py:201
  241.5 0.0 copy-start.1
  241.5 0.0 reduce-scatter.5.cloned.1.call-update
  241.5 81.4 %reduce-scatter.5.cloned.1.call-done = bf16[128,1536]{1,0:T(8,128)(2,1)} async-done(((bf16[2048,1536]{1,0:T(8,128)(2,1)}), bf16[128,1536]{1,0:T(8,128)(2,1)}) %reduce-scatter.5.cloned.1.call-update) | async-done | bytes 393232 | tf_op jit(solution)/shard_map/reduce_scatter | solution.py:285
  322.9 0.0 copy-done.1
  322.9 1.9 add_convert_fusion
  (11 shorter events, 0.1 us)
Async XLA Ops:
  6.5 33.7 %all-gather.4.cloned.1.call-start = ((), (), s32[]{:S(2)}) async-start(), calls=%async_computation.2 | async-start | bytes 3538944 | tf_op jit(solution)/shard_map/all_gather | solution.py:244
  9.6 78.5 %all-gather.6.cloned.1.call-start = ((), (), s32[]{:S(2)}) async-start(), calls=%async_computation.3 | async-start | bytes 2228224 | tf_op jit(solution)/shard_map/all_gather | solution.py:245
  10.4 139.0 %reduce-scatter.3.cloned.1.call-start = ((), (), s32[]{:S(2)}) async-start(), calls=%async_computation.4 | async-start | bytes 3538944 | tf_op jit(solution)/shard_map/reduce_scatter | solution.py:275
  46.8 41.4 %collective-permute-start = (bf16[1024,128]{1,0:T(8,128)(2,1)}, bf16[1024,128]{1,0:T(8,128)(2,1)S(1)}, u32[]{:S(2)}, u32[]{:S(2)}) collective-permute-start(bf16[1024,128]{1,0:T(8,128)(2,1)} %get-tuple-element.8.now_ref), channel_id=1, source_target_pairs={{0,8},{8,16},{16,24},{24,32},{32,40},{40,48},{48,56},{56,64},{64,7... | collective-permute-start | bytes 786440 | tf_op jit(solution)/shard_map/ppermute | solution.py:273
  88.2 0.7 copy-start.2
  112.8 36.5 %copy-start = (bf16[128,1536]{1,0:T(8,128)(2,1)S(1)}, bf16[128,1536]{1,0:T(8,128)(2,1)}, u32[]{:S(2)}) copy-start(bf16[128,1536]{1,0:T(8,128)(2,1)} %param.16) | copy-start | bytes 1179652
  112.8 37.7 %copy-start.3 = (f32[1536]{0:T(1024)S(1)}, f32[1536]{0:T(1024)}, u32[]{:S(2)}) copy-start(f32[1536]{0:T(1024)} %param.26) | copy-start | bytes 18436
  112.9 39.7 %copy-start.4 = (f32[128,8]{0,1:T(8,128)S(1)}, f32[128,8]{0,1:T(8,128)}, u32[]{:S(2)}) copy-start(f32[128,8]{0,1:T(8,128)} %param.28) | copy-start | bytes 12292
  112.9 39.7 %copy-start.5 = (s32[128,8]{0,1:T(8,128)S(1)}, s32[128,8]{0,1:T(8,128)}, u32[]{:S(2)}) copy-start(s32[128,8]{0,1:T(8,128)} %param.27) | copy-start | bytes 12292
  112.9 101.0 %all-gather.8.cloned.1.call-start = ((), (), s32[]{:S(2)}) async-start(), calls=%async_computation.5 | async-start | bytes 6684672 | tf_op jit(solution)/shard_map/all_gather | solution.py:282
  152.5 170.4 %reduce-scatter.5.cloned.1.call-start = ((), (), s32[]{:S(2)}) async-start(), calls=%async_computation.6 | async-start | bytes 6684672 | tf_op jit(solution)/shard_map/reduce_scatter | solution.py:285
  241.5 81.4 %copy-start.1 = (bf16[128,1536]{1,0:T(8,128)(2,1)S(1)}, bf16[128,1536]{1,0:T(8,128)(2,1)}, u32[]{:S(2)}) copy-start(bf16[128,1536]{1,0:T(8,128)(2,1)} %reduce-scatter.3.cloned.1.call-done) | copy-start | bytes 1179652
Sparse Core Ops, SparseCore 0:
  9.8 30.3 all-gather.3
  42.3 45.7 all-gather.5
  113.0 36.2 reduce-scatter.2
  152.6 61.1 all-gather.7
  241.7 81.2 reduce-scatter.4

commit v2 on v1

--- a/solution.py
+++ b/solution.py
@@ -180,13 +180,12 @@
     )(steps, used, fill, q, kv_prev, kv_now, cache, rows, w_out)
 
 
-def expert_kernel(first_ref, x_ref, gates_ref, wg_ref, wu_ref, wd_ref, out_ref):
+def expert_kernel(x_ref, gates_ref, wg_ref, wu_ref, wd_ref, out_ref):
     x = x_ref[...]
-    gates = gates_ref[...]
-    lane = lax.broadcasted_iota(jnp.int32, gates.shape, 1)
+    gates = jnp.concatenate([gates_ref[s].T for s in range(gates_ref.shape[0])], axis=0)
     total = jnp.zeros((x.shape[0], wd_ref.shape[2]), F32)
     for e in range(wg_ref.shape[0]):
-        gate = jnp.sum(jnp.where(lane == first_ref[0] + e, gates, 0.0), axis=1, keepdims=True)
+        gate = gates[:, e : e + 1]
         g = jnp.dot(x, wg_ref[e], preferred_element_type=F32)
         u = jnp.dot(x, wu_ref[e], preferred_element_type=F32)
         act = (g / (1.0 + jnp.exp(-g)) * u).astype(BF)
@@ -195,27 +194,553 @@
     out_ref[...] = total.astype(BF)
 
 
-def run_experts(first, x, gates, w_gate, w_up, w_down, rows=256):
+def run_experts(x, gates, w_gate, w_up, w_down, rows=256):
     length, width = x.shape
-    whole = lambda a: pl.BlockSpec(a.shape, lambda i, *_: (0,) * a.ndim, pipeline_mode=pl.Buffered(1))
+    whole = lambda a: pl.BlockSpec(a.shape, lambda i: (0,) * a.ndim, pipeline_mode=pl.Buffered(1))
     return pl.pallas_call(
         expert_kernel,
-        grid_spec=pltpu.PrefetchScalarGridSpec(
-            num_scalar_prefetch=1,
-            grid=(length // rows,),
-            in_specs=[
-                pl.BlockSpec((rows, width), lambda i, *_: (i, 0)),
-                pl.BlockSpec((rows, gates.shape[1]), lambda i, *_: (i, 0)),
-                whole(w_gate),
-                whole(w_up),
-                whole(w_down),
-            ],
-            out_specs=pl.BlockSpec((rows, width), lambda i, *_: (i, 0)),
-        ),
+        grid=(length // rows,),
+        in_specs=[
+            pl.BlockSpec((rows, width), lambda i: (i, 0)),
+            pl.BlockSpec((rows // gates.shape[2],) + gates.shape[1:], lambda i: (i, 0, 0)),
+            whole(w_gate),
+            whole(w_up),
+            whole(w_down),
+        ],
+        out_specs=pl.BlockSpec((rows, width), lambda i: (i, 0)),
         out_shape=jax.ShapeDtypeStruct((length, width), BF),
         compiler_params=pltpu.CompilerParams(vmem_limit_bytes=VMEM_CAP),
         name="experts",
-    )(first, x, gates, w_gate, w_up, w_down)
+    )(x, gates, w_gate, w_up, w_down)
+
+
+MESH_ID = pl.DeviceIdType.MESH
+
+
+def torus_messages():
+    keys = []
+    for half in (0, 1):
+        for sign in (1, -1):
+            keys.append(("near", half, 0, sign))
+            keys.append(("far", half, 0, sign))
+            for a in (0, -1, 1, 2):
+                keys.append(("side", half, a, sign))
+                keys.append(("last", half, a, sign))
+    return {key: i for i, key in enumerate(keys)}
+
+
+def place_of(place, dx, dy):
+    return ((place // 4 + dx + 4) % 4) * 4 + (place % 4 + dy + 4) % 4
+
+
+def torus_gather(own, out, rows, sends, receives, keys):
+    place, head = lax.axis_index("tok"), lax.axis_index("head")
+    half_rows, part = rows // 2, rows // 4
+    started = []
+
+    def unit(half, a, b):
+        return (a, b) if half == 0 else (b, a)
+
+    def copy(key, landing=False):
+        kind, half, a, sign = key
+        first = kind in ("near", "far")
+        if kind == "near":
+            source = (0, 0)
+        elif kind == "far":
+            source = (-sign, 0)
+        elif kind == "side":
+            source = (a, 0)
+        else:
+            source = (a, -sign)
+        begin, size = half * half_rows, half_rows
+        if kind in ("far", "last"):
+            begin, size = begin + (0 if sign == 1 else part), part
+        if landing:
+            source = (source[0] - sign, source[1]) if first else (source[0], source[1] - sign)
+        slot = place_of(place, *unit(half, *source))
+        step = unit(half, sign, 0) if first else unit(half, 0, sign)
+        target = out.at[slot, pl.ds(begin, size)]
+        if not landing and source == (0, 0):
+            src = own.at[pl.ds(begin, size)]
+        else:
+            src = target
+        return pltpu.make_async_remote_copy(
+            src_ref=src,
+            dst_ref=target,
+            send_sem=sends.at[keys[key]],
+            recv_sem=receives.at[keys[key]],
+            device_id=(place_of(place, *step), head),
+            device_id_type=MESH_ID,
+        )
+
+    def send(*key):
+        c = copy(key)
+        c.start()
+        started.append(c)
+
+    def arrive(*key):
+        copy(key, landing=True).wait_recv()
+
+    for sign in (1, -1):
+        for half in (0, 1):
+            send("near", half, 0, sign)
+    for sign in (1, -1):
+        for half in (0, 1):
+            send("side", half, 0, sign)
+    yield
+    for sign in (1, -1):
+        for half in (0, 1):
+            arrive("near", half, 0, sign)
+            send("far", half, 0, sign)
+            send("side", half, -sign, 1)
+            send("side", half, -sign, -1)
+    yield
+    for sign in (1, -1):
+        for half in (0, 1):
+            arrive("side", half, 0, sign)
+            send("last", half, 0, sign)
+    yield
+    for half in (0, 1):
+        for sign in (1, -1):
+            arrive("far", half, 0, sign)
+        for sign in (1, -1):
+            send("side", half, 2, sign)
+    yield
+    for a in (-1, 1, 2):
+        for sign in (1, -1):
+            for half in (0, 1):
+                arrive("side", half, a, sign)
+                send("last", half, a, sign)
+        yield
+    for a in (0, -1, 1, 2):
+        for half in (0, 1):
+            for sign in (1, -1):
+                arrive("last", half, a, sign)
+    for c in started:
+        c.wait_send()
+    yield
+
+
+def greet(peers):
+    barrier = pltpu.get_barrier_semaphore()
+    for peer in peers:
+        pl.semaphore_signal(barrier, inc=1, device_id=peer, device_id_type=MESH_ID)
+    pl.semaphore_wait(barrier, len(peers))
+
+
+def torus_peers():
+    place, head = lax.axis_index("tok"), lax.axis_index("head")
+    return [(place_of(place, *s), head) for s in ((1, 0), (-1, 0), (0, 1), (0, -1))]
+
+
+def scatter_messages():
+    keys = []
+    for half in (0, 1):
+        for a in (2, -1, 1, 0):
+            for sign in (1, -1):
+                for kind in ("far", "plain", "added"):
+                    keys.append((kind, half, a, sign))
+        for sign in (1, -1):
+            for kind in ("far2", "plain2", "added2"):
+                keys.append((kind, half, 0, sign))
+    return {key: i for i, key in enumerate(keys)}
+
+
+def torus_scatter(parts, land, rows, sends, receives, keys):
+    place, head = lax.axis_index("tok"), lax.axis_index("head")
+    half_rows, part = rows // 2, rows // 4
+    started = []
+
+    def unit(half, a, b):
+        return (a, b) if half == 0 else (b, a)
+
+    def spot(key):
+        kind, half, a, sign = key
+        second = kind.endswith("2")
+        base = half * half_rows
+        low, high = pl.ds(base, part), pl.ds(base + part, part)
+        with_far, plain = (low, high) if sign == 1 else (high, low)
+        distance = 2 if kind.startswith("far") else sign
+        offset = (distance, 0) if second else (a, distance)
+        rows_of = plain if kind.startswith("plain") else with_far
+        return place_of(place, *unit(half, *offset)), rows_of
+
+    def copy(key):
+        kind, half, a, sign = key
+        slot, rows_of = spot(key)
+        step = unit(half, sign, 0) if kind.endswith("2") else unit(half, 0, sign)
+        return pltpu.make_async_remote_copy(
+            src_ref=parts.at[slot, rows_of],
+            dst_ref=land.at[keys[key]],
+            send_sem=sends.at[keys[key]],
+            recv_sem=receives.at[keys[key]],
+            device_id=(place_of(place, *step), head),
+            device_id_type=MESH_ID,
+        )
+
+    def send(*key):
+        c = copy(key)
+        c.start()
+        started.append(c)
+
+    def add(key, slot, rows_of):
+        copy(key).wait_recv()
+        parts[slot, rows_of] = (
+            parts[slot, rows_of].astype(F32) + land[keys[key]].astype(F32)
+        ).astype(parts.dtype)
+
+    order = (2, -1, 1, 0)
+    for a in order:
+        for sign in (1, -1):
+            for half in (0, 1):
+                send("far", half, a, sign)
+        for sign in (1, -1):
+            for half in (0, 1):
+                send("plain", half, a, sign)
+        yield
+    for step in range(len(order) + 1):
+        if step < len(order):
+            a = order[step]
+            for sign in (1, -1):
+                for half in (0, 1):
+                    slot, rows_of = spot(("added", half, a, sign))
+                    add(("far", half, a, sign), slot, rows_of)
+                    send("added", half, a, sign)
+            yield
+        if step > 0:
+            a = order[step - 1]
+            for half in (0, 1):
+                slot = place_of(place, *unit(half, a, 0))
+                for sign in (1, -1):
+                    for kind in ("plain", "added"):
+                        _, rows_of = spot((kind, half, a, sign))
+                        add((kind, half, a, sign), slot, rows_of)
+                if a == 2:
+                    for sign in (1, -1):
+                        send("far2", half, 0, sign)
+                elif a != 0:
+                    send("plain2", half, 0, a)
+            yield
+        if step == 3:
+            for half in (0, 1):
+                for sign in (1, -1):
+                    slot, rows_of = spot(("added2", half, 0, sign))
+                    add(("far2", half, 0, sign), slot, rows_of)
+                    send("added2", half, 0, sign)
+            yield
+    for half in (0, 1):
+        for sign in (1, -1):
+            for kind in ("plain2", "added2"):
+                _, rows_of = spot((kind, half, 0, sign))
+                add((kind, half, 0, sign), place, rows_of)
+    for c in started:
+        c.wait_send()
+    yield
+
+
+def scatter_kernel(x_ref, hidden_ref, out_ref, parts, land, sends, receives, own_sems):
+    keys = scatter_messages()
+    loads = [pltpu.make_async_copy(x_ref.at[s], parts.at[s], own_sems.at[s]) for s in range(parts.shape[0])]
+    for c in loads:
+        c.start()
+    greet(torus_peers())
+    for c in loads:
+        c.wait()
+    for _ in torus_scatter(parts, land, parts.shape[1], sends, receives, keys):
+        pass
+    out_ref[...] = (hidden_ref[...] + parts[lax.axis_index("tok")].astype(F32)).astype(out_ref.dtype)
+
+
+def scatter_tok(x, hidden, collective_id):
+    count = len(scatter_messages())
+    _, rows, width = x.shape
+    return pl.pallas_call(
+        scatter_kernel,
+        in_specs=[pl.BlockSpec(memory_space=pl.ANY), pl.BlockSpec(memory_space=pltpu.VMEM)],
+        out_specs=pl.BlockSpec(memory_space=pltpu.VMEM),
+        out_shape=jax.ShapeDtypeStruct((rows, width), x.dtype),
+        scratch_shapes=[
+            pltpu.VMEM(x.shape, x.dtype),
+            pltpu.VMEM((count, rows // 4, width), x.dtype),
+            pltpu.SemaphoreType.DMA((count,)),
+            pltpu.SemaphoreType.DMA((count,)),
+            pltpu.SemaphoreType.DMA((16,)),
+        ],
+        compiler_params=pltpu.CompilerParams(
+            collective_id=collective_id, has_side_effects=True, vmem_limit_bytes=VMEM_CAP
+        ),
+        name="scatter_tok",
+    )(x, hidden)
+
+
+def ring_messages(kinds):
+    return {key: i for i, key in enumerate(kinds)}
+
+
+GATHER_RING = ring_messages(
+    [("near", 1), ("near", -1), ("far", 1), ("far", -1), ("pair", 0), ("pair", 1), ("pair", -1), ("half", 1), ("half", -1)]
+)
+SCATTER_RING = ring_messages(
+    [("pair", 2), ("pair", 1), ("pair", -1), ("pair", 0)]
+    + [(kind, sign) for kind in ("far", "plain", "added") for sign in (1, -1)]
+)
+
+
+def head_of(head, dz, flip=0):
+    core = head % 2
+    return ((head // 2 + dz + 4) % 4) * 2 + (core + flip) % 2
+
+
+def ring_peers():
+    place, head = lax.axis_index("tok"), lax.axis_index("head")
+    return [(place, head_of(head, 1)), (place, head_of(head, -1)), (place, head_of(head, 0, 1))]
+
+
+def ring_gather(own, out, rows, sends, receives, keys):
+    place, head = lax.axis_index("tok"), lax.axis_index("head")
+    started = []
+
+    def copy(key, landing=False):
+        kind, value = key
+        begin, size = 0, rows
+        if kind in ("far", "half"):
+            size = rows // 2
+            begin = 0 if value == 1 else size
+        dz = {"near": 0, "far": -value, "pair": value, "half": 2}[kind]
+        crossing = kind in ("pair", "half")
+        if landing:
+            slot = head_of(head, dz, 1) if crossing else head_of(head, dz - value)
+        else:
+            slot = head_of(head, dz)
+        target = out.at[slot, pl.ds(begin, size)]
+        src = own.at[pl.ds(begin, size)] if not landing and dz == 0 else target
+        peer = head_of(head, 0, 1) if crossing else head_of(head, value)
+        return pltpu.make_async_remote_copy(
+            src_ref=src,
+            dst_ref=target,
+            send_sem=sends.at[keys[key]],
+            recv_sem=receives.at[keys[key]],
+            device_id=(place, peer),
+            device_id_type=MESH_ID,
+        )
+
+    def send(*key):
+        c = copy(key)
+        c.start()
+        started.append(c)
+
+    def arrive(*key):
+        copy(key, landing=True).wait_recv()
+
+    send("near", 1)
+    send("near", -1)
+    send("pair", 0)
+    yield
+    for sign in (1, -1):
+        arrive("near", sign)
+        send("far", sign)
+        send("pair", -sign)
+    yield
+    for sign in (1, -1):
+        arrive("far", sign)
+        send("half", sign)
+    yield
+    for dz in (0, 1, -1):
+        arrive("pair", dz)
+    for sign in (1, -1):
+        arrive("half", sign)
+    for c in started:
+        c.wait_send()
+    yield
+
+
+def opening_kernel(x_ref, cache_ref, gates_ref, x_out, cache_out, gates_out, ts, tr, hs, hr, gs, gr, own_sems):
+    place, head = lax.axis_index("tok"), lax.axis_index("head")
+    count = gates_ref.shape[0]
+    others = [((place + d) % count, head) for d in range(1, count)]
+    greet(others + ring_peers())
+    mine = [
+        pltpu.make_async_copy(x_ref, x_out.at[head], own_sems.at[0]),
+        pltpu.make_async_copy(cache_ref, cache_out.at[place], own_sems.at[1]),
+        pltpu.make_async_copy(gates_ref.at[place], gates_out.at[place], own_sems.at[2]),
+    ]
+    one = ring_gather(x_ref, x_out, x_ref.shape[0], hs, hr, GATHER_RING)
+    two = torus_gather(cache_ref, cache_out, cache_ref.shape[0], ts, tr, torus_messages())
+
+    def gate_copy(d, landing=False):
+        target = (place + d) % count
+        slot = (place - d + count) % count if landing else place
+        return pltpu.make_async_remote_copy(
+            src_ref=gates_ref.at[target],
+            dst_ref=gates_out.at[slot],
+            send_sem=gs.at[d],
+            recv_sem=gr.at[d],
+            device_id=(target, head),
+            device_id_type=MESH_ID,
+        )
+
+    next(one)
+    next(two)
+    for c in mine:
+        c.start()
+    for d in range(1, count):
+        gate_copy(d).start()
+    for _ in range(2):
+        next(one)
+        next(two)
+    for _ in two:
+        pass
+    for _ in one:
+        pass
+    for d in range(1, count):
+        gate_copy(d, True).wait_recv()
+    for d in range(1, count):
+        gate_copy(d).wait_send()
+    for c in mine:
+        c.wait()
+
+
+def opening(x, cache, gates, collective_id):
+    t, r, n = len(torus_messages()), len(GATHER_RING), gates.shape[0]
+    dma = pltpu.SemaphoreType.DMA
+    return pl.pallas_call(
+        opening_kernel,
+        in_specs=[pl.BlockSpec(memory_space=pltpu.VMEM)] * 3,
+        out_specs=[pl.BlockSpec(memory_space=pl.ANY)] * 3,
+        out_shape=[
+            jax.ShapeDtypeStruct((8,) + x.shape, x.dtype),
+            jax.ShapeDtypeStruct((n,) + cache.shape, cache.dtype),
+            jax.ShapeDtypeStruct(gates.shape, gates.dtype),
+        ],
+        scratch_shapes=[dma((t,)), dma((t,)), dma((r,)), dma((r,)), dma((n,)), dma((n,)), dma((3,))],
+        compiler_params=pltpu.CompilerParams(collective_id=collective_id, has_side_effects=True),
+        name="opening",
+    )(x, cache, gates)
+
+
+def ring_scatter(parts, pair_land, land, rows, sends, receives, keys):
+    place, head = lax.axis_index("tok"), lax.axis_index("head")
+    started = []
+    low, high = pl.ds(0, rows // 2), pl.ds(rows // 2, rows // 2)
+
+    def spot(key):
+        kind, value = key
+        if kind == "far":
+            return head_of(head, 2), (low if value == 1 else high)
+        if kind == "plain":
+            return head_of(head, value), (high if value == 1 else low)
+        return head_of(head, value), (low if value == 1 else high)
+
+    def copy(key):
+        kind, value = key
+        if kind == "pair":
+            src, dst = parts.at[head_of(head, value, 1)], pair_land.at[keys[key]]
+            peer = head_of(head, 0, 1)
+        else:
+            slot, rows_of = spot(key)
+            src, dst = parts.at[slot, rows_of], land.at[keys[key] - 4]
+            peer = head_of(head, value)
+        return pltpu.make_async_remote_copy(
+            src_ref=src,
+            dst_ref=dst,
+            send_sem=sends.at[keys[key]],
+            recv_sem=receives.at[keys[key]],
+            device_id=(place, peer),
+            device_id_type=MESH_ID,
+        )
+
+    def send(*key):
+        c = copy(key)
+        c.start()
+        started.append(c)
+
+    def add(key, slot, rows_of, buffer, index):
+        copy(key).wait_recv()
+        parts[slot, rows_of] = (parts[slot, rows_of].astype(F32) + buffer[index].astype(F32)).astype(parts.dtype)
+
+    def add_pair(dz):
+        key = ("pair", dz)
+        add(key, head_of(head, dz), pl.ds(0, rows), pair_land, keys[key])
+
+    for dz in (2, 1, -1, 0):
+        send("pair", dz)
+    add_pair(2)
+    for sign in (1, -1):
+        send("far", sign)
+    for sign in (1, -1):
+        add_pair(sign)
+        send("plain", sign)
+    add_pair(0)
+    for sign in (1, -1):
+        key = ("far", sign)
+        slot, rows_of = spot(("added", sign))
+        add(key, slot, rows_of, land, keys[key] - 4)
+        send("added", sign)
+    for kind in ("plain", "added"):
+        for sign in (1, -1):
+            key = (kind, sign)
+            _, rows_of = spot(key)
+            add(key, head, rows_of, land, keys[key] - 4)
+    for c in started:
+        c.wait_send()
+
+
+def settle_kernel(
+    part_ref, tokens_ref, gain_ref, hidden_ref, out_ref, parts, pair_land, land, normed, rs, rr, ts, tr, own_sems
+):
+    place, head = lax.axis_index("tok"), lax.axis_index("head")
+    rows = tokens_ref.shape[0]
+    loads = [
+        pltpu.make_async_copy(part_ref.at[pl.ds(h * rows, rows)], parts.at[h], own_sems.at[h]) for h in range(8)
+    ]
+    for c in loads:
+        c.start()
+    greet(torus_peers() + ring_peers())
+    for c in loads:
+        c.wait()
+    ring_scatter(parts, pair_land, land, rows, rs, rr, SCATTER_RING)
+    hidden = tokens_ref[...].astype(F32) + parts[head].astype(F32)
+    hidden_ref[...] = hidden
+    normed[...] = rms_scale(hidden, gain_ref[...]).astype(normed.dtype)
+    mine = pltpu.make_async_copy(normed, out_ref.at[place], own_sems.at[8])
+    mine.start()
+    for _ in torus_gather(normed, out_ref, rows, ts, tr, torus_messages()):
+        pass
+    mine.wait()
+
+
+def settle(partial, tokens, gain, collective_id):
+    rows, width = tokens.shape
+    t, r = len(torus_messages()), len(SCATTER_RING)
+    dma = pltpu.SemaphoreType.DMA
+    return pl.pallas_call(
+        settle_kernel,
+        in_specs=[
+            pl.BlockSpec(memory_space=pl.ANY),
+            pl.BlockSpec(memory_space=pltpu.VMEM),
+            pl.BlockSpec(memory_space=pltpu.VMEM),
+        ],
+        out_specs=[pl.BlockSpec(memory_space=pltpu.VMEM), pl.BlockSpec(memory_space=pl.ANY)],
+        out_shape=[
+            jax.ShapeDtypeStruct((rows, width), F32),
+            jax.ShapeDtypeStruct((16, rows, width), BF),
+        ],
+        scratch_shapes=[
+            pltpu.VMEM((8, rows, width), BF),
+            pltpu.VMEM((4, rows, width), BF),
+            pltpu.VMEM((6, rows // 2, width), BF),
+            pltpu.VMEM((rows, width), BF),
+            dma((r,)),
+            dma((r,)),
+            dma((t,)),
+            dma((t,)),
+            dma((9,)),
+        ],
+        compiler_params=pltpu.CompilerParams(
+            collective_id=collective_id, has_side_effects=True, vmem_limit_bytes=VMEM_CAP
+        ),
+        name="settle",
+    )(partial, tokens, gain)
 
 
 def local(
@@ -241,8 +766,14 @@
     place = lax.axis_index("tok")
     row_len = tokens.shape[0] * head_count
     normed = rms_scale(tokens, attn_gain).astype(BF)
-    gathered = lax.all_gather(normed, "head", axis=0, tiled=True)
-    cache = lax.all_gather(prefix_cache, "tok", axis=0, tiled=True)
+    exp_local = w_gate.shape[0]
+    experts = jnp.arange(EXPERTS, dtype=jnp.int32)[:, None, None]
+    gates = jnp.sum(jnp.where(routes.T[None] == experts, route_gates.T[None], 0.0), axis=1)
+    gates = gates.reshape(tok_count, exp_local, -1)
+    gates = jnp.concatenate([gates, jnp.zeros((tok_count, 8 - exp_local, gates.shape[2]), F32)], axis=1)
+    gathered, cache, gates_all = opening(normed, prefix_cache, gates, 1)
+    gathered = gathered.reshape(row_len, -1)
+    cache = cache.reshape(-1, cache.shape[-1])
 
     padded = jnp.concatenate([jnp.full((row_len,), -1, jnp.int32), segments])
     window = lax.dynamic_slice_in_dim(padded, place * row_len, 2 * row_len, 0)
@@ -272,18 +803,9 @@
     q, kv_now = project(gathered, w_query, w_keyval, cos, sin)
     kv_prev = lax.ppermute(kv_now, "tok", [(i, i + 1) for i in range(tok_count - 1)])
     partial = attend(q, kv_prev, kv_now, cache, rows, steps, used, slab_fill, w_out)
-    attended = lax.psum_scatter(partial, "head", scatter_dimension=0, tiled=True).astype(F32)
-    hidden = tokens.astype(F32) + attended
-    expert_in = rms_scale(hidden, ffn_gain).astype(BF)
-
-    experts = jnp.arange(EXPERTS, dtype=jnp.int32)
-    gates = jnp.sum(jnp.where(routes[:, :, None] == experts, route_gates[:, :, None], 0.0), axis=1)
-    gates_all = lax.all_gather(gates, "tok", axis=0, tiled=True)
-    arrived = lax.all_gather(expert_in, "tok", axis=0, tiled=True)
-    first = (place * w_gate.shape[0]).astype(jnp.int32).reshape(1)
-    answered = run_experts(first, arrived, gates_all, w_gate, w_up, w_down)
-    mixture = lax.psum_scatter(answered, "tok", scatter_dimension=0, tiled=True)
-    return (hidden + mixture.astype(F32)).astype(BF)
+    hidden, arrived = settle(partial, tokens, ffn_gain[None], 2)
+    answered = run_experts(arrived.reshape(-1, arrived.shape[-1]), gates_all, w_gate, w_up, w_down)
+    return scatter_tok(answered.reshape(arrived.shape), hidden, 3)
 
 
 def solution(mesh):

time: 332 us -> 218 us (0.66)
  waiting for transfers between devices: 207 us -> 0.62 us
  Pallas kernels: 58.2 us -> 195 us
  blocking collectives: 28.5 us -> 0 us
  between operations: 13.3 us -> 0.1 us
  other arithmetic: 15.7 us -> 11.4 us
    pallas_call x1 -> x4, Pallas kernels: 27.6 us -> 166 us  [the longest x1 63 us: settle(): pl.pallas_call(settle_kernel, in_specs=[pl.BlockSpec(memory_space=pl.ANY)...]
    reduce_scatter x2 -> x0, waiting for transfers between devices: 118 us -> none  [the longest x1 81.4 us: local(): mixture = lax.psum_scatter(answered, 'tok', scatter_dimension=0, tiled=True)]
    all_gather x3 -> x0, waiting for transfers between devices: 88.9 us -> none  [the longest x1 36.6 us: local(): cache = lax.all_gather(prefix_cache, 'tok', axis=0, tiled=True)]
    all_gather x1 -> x0, blocking collectives: 28.5 us -> none  [local(): gates_all = lax.all_gather(gates, 'tok', axis=0, tiled=True)]
    convert_element_type x2 -> x0, other arithmetic: 3.78 us -> none  [the longest x1 1.9 us: local(): expert_in = rms_scale(hidden, ffn_gain).astype(BF)]
  transfers between devices with their start and end apart: 6 -> 1, of which waited for: 5 -> 1; matrix products, arithmetic and copies ran while one was open for 4% -> 2% of each run, Pallas kernels for 2% -> 0%
where the time goes in v2:
time: 218 us
  Pallas kernels  195 us (89%)
  other arithmetic  11.4 us (5%)
  local copies, waits for them, and re-layouts  7.61 us (3%)
  starting transfers between devices  2.78 us (1%)
    pallas_call x1, Pallas kernels, settle(): pl.pallas_call(settle_kernel, in_specs=[pl.BlockSpec(memory_space=pl.ANY)...  63 us
    pallas_call x1, Pallas kernels, scatter_tok(): pl.pallas_call(scatter_kernel, in_specs=[pl.BlockSpec(memory_space=pl.ANY...  41.5 us
    pallas_call x1, Pallas kernels, opening(): pl.pallas_call(opening_kernel, in_specs=[pl.BlockSpec(memory_space=pltpu....  33.6 us
    pallas_call x1, Pallas kernels, run_experts(): pl.pallas_call(expert_kernel, grid=(length // rows,), in_specs=[pl.BlockS...  27.6 us
    pallas_call x1, Pallas kernels, attend(): pl.pallas_call(attend_kernel, grid_spec=pltpu.PrefetchScalarGridSpec(num_...  22.8 us
    pallas_call x1, Pallas kernels, project(): pl.pallas_call(project_kernel, grid=(length // rows,), in_specs=[pl.Block...  6.61 us
    unnamed x6, local copies, waits for them, and re-layouts  4.72 us
  transfers between devices with their start and end apart: 1, of which 1 were waited for; matrix products, arithmetic and copies ran while one was open for 2% of the time, Pallas kernels for 0%

profile of v2, /device:TPU:0, one launch (start us, length us, event | category | flops | bytes accessed | tf_op | source)
XLA Modules:
  0.0 217.6 jit_solution(9366695882288058052)
XLA Ops:
  0.0 1.2 fusion
  1.2 0.7 pad_dynamic-slice_fusion.1
  1.9 0.7 pad_dynamic-slice_fusion
  2.6 0.2 convert_reduce_fusion
  2.8 0.8 select_reduce_fusion.5
  3.5 0.7 select_reduce_fusion.4
  4.3 0.1 select_reduce_fusion
  4.4 2.2 %copy.25.wq_ref = bf16[1536,192]{1,0:T(8,128)(2,1)} copy(bf16[1536,192]{0,1:T(8,128)(2,1)} %param.23) | data formatting | bytes 1179648 | tf_op args[7]
  6.7 0.7 select_reduce_fusion.1
  7.4 0.6 concatenate.14.gates_ref
  8.1 1.9 fusion.2.x_ref
  10.0 3.1 %negate_select_fusion = (f32[1024,128]{1,0:T(8,128)}, f32[1024,128]{1,0:T(8,128)}) fusion(f32[128]{0:T(128)S(1)} %fusion.22, f32[1024]{0:T(1024)S(1)} %fusion.10, pred[128]{0:T(512)(128)(4,1)S(1)} %fusion.23), kind=kLoop, calls=%fused_computation.7 | loop fusion | flops 393216 | bytes 1053312 | tf_op jit(solution)/shard_map/jit(_where)/select_n | solution.py:788
  13.0 0.0 copy-start.1
  13.0 33.6 %opening.1 = (bf16[8,128,1536]{2,1,0:T(8,128)(2,1)}, bf16[16,512,128]{2,1,0:T(8,128)(2,1)}, f32[16,8,128]{2,1,0:T(8,128)}) custom-call(bf16[128,1536]{1,0:T(8,128)(2,1)} %fusion.2.x_ref, bf16[512,128]{1,0:T(8,128)(2,1)} %cache_ref.1, f32[16,8,128]{2,1,0:T(8,128)} %concatenate.14.gates_ref), custom_call_target="tpu_custom_call" | custom-call | tf_op jit(solution)/shard_map/opening/pallas_call | solution.py:606
  46.6 6.6 %project.1 = (bf16[3,1024,128]{2,1,0:T(8,128)(2,1)}, bf16[1024,128]{1,0:T(8,128)(2,1)}) custom-call(bf16[1024,1536]{1,0:T(8,128)(2,1)} %bitcast.31, bf16[1536,192]{1,0:T(8,128)(2,1)} %copy.25.wq_ref, bf16[1536,128]{1,0:T(8,128)(2,1)} %wkv_ref.1, f32[1024,128]{1,0:T(8,128)} %get-tuple-element.20.cos_ref, f32[1024,128]{1,0:T(8,128)} %get-tuple-element.19.sin_ref), custom_call_target="tpu_custom_call" | custom-call | tf_op jit(solution)/shard_map/project/pallas_call | solution.py:67
  53.2 2.8 %collective-permute-start = (bf16[1024,128]{1,0:T(8,128)(2,1)}, bf16[1024,128]{1,0:T(8,128)(2,1)S(1)}, u32[]{:S(2)}, u32[]{:S(2)}) collective-permute-start(bf16[1024,128]{1,0:T(8,128)(2,1)} %get-tuple-element.14.now_ref), channel_id=1, source_target_pairs={{0,8},{8,16},{16,24},{24,32},{32,40},{40,48},{48,56},{56,64},{64,7... | collective-permute-start | bytes 786440 | tf_op jit(solution)/shard_map/ppermute | solution.py:804
  56.1 0.2 convert_reduce_fusion.1
  56.3 0.1 reduce_sum.90
  56.4 0.1 and_select_fusion.2
  56.5 0.1 slice_reduce_fusion
  56.6 0.6 and_select_fusion.5.steps_ref
  57.2 0.1 select_reduce_fusion.3
  57.3 0.1 copy.24
  57.4 0.2 select_reduce_fusion.2
  57.6 0.7 pad_add_fusion.used_ref
  58.2 0.1 pad.4.clone
  58.3 0.0 copy-done.1
  58.3 0.6 broadcast_in_dim.112.gain_ref
  58.9 0.7 add_add_fusion.rows_ref
  59.6 0.6 collective-permute-done.prev_ref
  60.2 0.0 copy-start
  60.2 0.7 copy-done
  60.9 22.8 %attend.1.part_ref = bf16[1024,1536]{1,0:T(8,128)(2,1)} custom-call(s32[8]{0:T(128)} %and_select_fusion.5.steps_ref, s32[8,17]{1,0:T(8,128)} %pad_add_fusion.used_ref, s32[16]{0:T(128)} %fill_ref.1, bf16[3,1024,128]{2,1,0:T(8,128)(2,1)} %get-tuple-element.13.q_ref, bf16[1024,128]{1,0:T(8,128)(2,1)} %copy-done, bf16[1024,128]{1,0:T(8,128)(2,1)} %get-tuple-element.14.now_ref, ...), custom_call_target="tpu_custom_call" | custom-call | tf_op jit(solution)/shard_map/attend/pallas_call | solution.py:161
  83.8 63.0 %settle.1 = (f32[128,1536]{1,0:T(8,128)}, bf16[16,128,1536]{2,1,0:T(8,128)(2,1)}) custom-call(bf16[1024,1536]{1,0:T(8,128)(2,1)} %attend.1.part_ref, bf16[128,1536]{1,0:T(8,128)(2,1)} %tokens_ref.1, f32[1,1536]{1,0:T(1,128)} %broadcast_in_dim.112.gain_ref), custom_call_target="tpu_custom_call" | custom-call | tf_op jit(solution)/shard_map/settle/pallas_call | solution.py:716
  146.7 27.6 %experts.1 = bf16[2048,1536]{1,0:T(8,128)(2,1)} custom-call(bf16[2048,1536]{1,0:T(8,128)(2,1)} %bitcast.30, f32[16,8,128]{2,1,0:T(8,128)} %get-tuple-element.17.gates_ref, bf16[2,1536,512]{2,1,0:T(8,128)(2,1)} %wg_ref.1, bf16[2,1536,512]{2,1,0:T(8,128)(2,1)} %wu_ref.1, bf16[2,512,1536]{2,1,0:T(8,128)(2,1)} %wd_ref.1), custom_call_target="tpu_custom_call" | custom-call | tf_op jit(solution)/shard_map/experts/pallas_call | solution.py:200
  174.3 41.5 %scatter_tok.1 = bf16[128,1536]{1,0:T(8,128)(2,1)} custom-call(bf16[16,128,1536]{2,1,0:T(8,128)(2,1)} %bitcast.29, f32[128,1536]{1,0:T(8,128)} %get-tuple-element.18.hidden_ref), custom_call_target="tpu_custom_call" | custom-call | tf_op jit(solution)/shard_map/scatter_tok/pallas_call | solution.py:457
  215.8 1.8 copy.27
  (9 shorter events, 0.1 us)
Async XLA Ops:
  13.0 45.3 %copy-start.1 = (f32[1536]{0:T(1024)S(1)}, f32[1536]{0:T(1024)}, u32[]{:S(2)}) copy-start(f32[1536]{0:T(1024)} %param.26) | copy-start | bytes 18436
  53.2 7.0 %collective-permute-start = (bf16[1024,128]{1,0:T(8,128)(2,1)}, bf16[1024,128]{1,0:T(8,128)(2,1)S(1)}, u32[]{:S(2)}, u32[]{:S(2)}) collective-permute-start(bf16[1024,128]{1,0:T(8,128)(2,1)} %get-tuple-element.14.now_ref), channel_id=1, source_target_pairs={{0,8},{8,16},{16,24},{24,32},{32,40},{40,48},{48,56},{56,64},{64,7... | collective-permute-start | bytes 786440 | tf_op jit(solution)/shard_map/ppermute | solution.py:804
  60.2 0.7 copy-start

commit v3 on v2

--- a/solution.py
+++ b/solution.py
@@ -37,68 +37,34 @@
     return mine // (16 * 1024), (mine // 1024) % 16, mine % 1024
 
 
-def project_kernel(x_ref, wq_ref, wkv_ref, cos_ref, sin_ref, q_ref, kv_ref):
-    x = x_ref[...]
-    heads = wq_ref.shape[1] // HS
-    pq = jnp.dot(x, wq_ref[...], preferred_element_type=F32)
-    pkv = jnp.dot(x, wkv_ref[...], preferred_element_type=F32)
-    both = jnp.concatenate([pq, pkv], axis=1)
+def turn(x, wq, wkv, cos, sin):
+    both = jnp.concatenate(
+        [
+            lax.dot_general(x, wq, (((1,), (1,)), ((), ())), preferred_element_type=F32),
+            jnp.dot(x, wkv, preferred_element_type=F32),
+        ],
+        axis=1,
+    )
     width = both.shape[1]
     lane = lax.broadcasted_iota(jnp.int32, both.shape, 1)
     swapped = jnp.where(
         lane % HS < HS // 2,
-        pltpu.roll(both, width - HS // 2, 1),
+        -pltpu.roll(both, width - HS // 2, 1),
         pltpu.roll(both, HS // 2, 1),
     )
     copies = -(-width // 128)
-    cos = jnp.concatenate([cos_ref[...]] * copies, axis=1)[:, :width]
-    sin = jnp.concatenate([sin_ref[...]] * copies, axis=1)[:, :width]
-    turned = jnp.where(lane < (heads + 1) * HS, both * cos + swapped * sin, both).astype(BF)
-    pad = jnp.zeros((x.shape[0], HS), BF)
-    for head in range(heads):
-        q_ref[head] = jnp.concatenate([turned[:, head * HS : (head + 1) * HS], pad], axis=1)
-    kv_ref[...] = turned[:, heads * HS :]
-
-
-def project(x, w_query, w_keyval, cos, sin, rows=256):
-    length = x.shape[0]
-    heads = w_query.shape[1] // HS
-    whole = lambda a: pl.BlockSpec(a.shape, lambda i: (0,) * a.ndim)
-    return pl.pallas_call(
-        project_kernel,
-        grid=(length // rows,),
-        in_specs=[
-            pl.BlockSpec((rows, x.shape[1]), lambda i: (i, 0)),
-            whole(w_query),
-            whole(w_keyval),
-            pl.BlockSpec((rows, 128), lambda i: (i, 0)),
-            pl.BlockSpec((rows, 128), lambda i: (i, 0)),
-        ],
-        out_specs=[
-            pl.BlockSpec((heads, rows, 128), lambda i: (0, i, 0)),
-            pl.BlockSpec((rows, 128), lambda i: (i, 0)),
-        ],
-        out_shape=[
-            jax.ShapeDtypeStruct((heads, length, 128), BF),
-            jax.ShapeDtypeStruct((length, 128), BF),
-        ],
-        compiler_params=pltpu.CompilerParams(vmem_limit_bytes=VMEM_CAP),
-        name="project",
-    )(x, w_query, w_keyval, cos, sin)
+    cos = jnp.concatenate([cos] * copies, axis=1)[:, :width]
+    sin = jnp.concatenate([sin] * copies, axis=1)[:, :width]
+    return jnp.where(lane < wq.shape[0] + HS, both * cos + swapped * sin, both).astype(BF)
 
 
 def attend_kernel(
-    steps_ref, used_ref, fill_ref, q_ref, prev_ref, now_ref, cache_ref, rows_ref, wout_ref, out_ref, near_ref
+    steps_ref, used_ref, fill_ref, q_ref, near_ref, cache_ref, rows_ref, wout_ref, out_ref
 ):
     block = pl.program_id(0)
     heads, span = q_ref.shape[0], q_ref.shape[1]
-    row_len = now_ref.shape[0]
+    row_len = near_ref.shape[0] // 2
     scale = HS ** (-0.5) * LOG2E
-
-    @pl.when(block == 0)
-    def _():
-        near_ref[:row_len] = prev_ref[...]
-        near_ref[row_len:] = now_ref[...]
 
     queries = jnp.concatenate([q_ref[h] for h in range(heads)], axis=0)
     begins = jnp.concatenate([rows_ref[0:1]] * heads, axis=1)
@@ -155,7 +121,7 @@
     out_ref[...] = jnp.dot(mixed.astype(BF), wout_ref[...], preferred_element_type=F32).astype(BF)
 
 
-def attend(q, kv_prev, kv_now, cache, rows, steps, used, fill, w_out, span=128):
+def attend(q, near, cache, rows, steps, used, fill, w_out, span=128):
     heads, length, _ = q.shape
     whole = lambda a: pl.BlockSpec(a.shape, lambda i, *_: (0,) * a.ndim)
     return pl.pallas_call(
@@ -165,53 +131,17 @@
             grid=(length // span,),
             in_specs=[
                 pl.BlockSpec((heads, span, 128), lambda i, *_: (0, i, 0)),
-                whole(kv_prev),
-                whole(kv_now),
+                whole(near),
                 whole(cache),
                 pl.BlockSpec((8, span), lambda i, *_: (0, i)),
                 whole(w_out),
             ],
             out_specs=pl.BlockSpec((span, w_out.shape[1]), lambda i, *_: (i, 0)),
-            scratch_shapes=[pltpu.VMEM((2 * length, 128), BF)],
         ),
         out_shape=jax.ShapeDtypeStruct((length, w_out.shape[1]), BF),
         compiler_params=pltpu.CompilerParams(vmem_limit_bytes=VMEM_CAP),
         name="attend",
-    )(steps, used, fill, q, kv_prev, kv_now, cache, rows, w_out)
-
-
-def expert_kernel(x_ref, gates_ref, wg_ref, wu_ref, wd_ref, out_ref):
-    x = x_ref[...]
-    gates = jnp.concatenate([gates_ref[s].T for s in range(gates_ref.shape[0])], axis=0)
-    total = jnp.zeros((x.shape[0], wd_ref.shape[2]), F32)
-    for e in range(wg_ref.shape[0]):
-        gate = gates[:, e : e + 1]
-        g = jnp.dot(x, wg_ref[e], preferred_element_type=F32)
-        u = jnp.dot(x, wu_ref[e], preferred_element_type=F32)
-        act = (g / (1.0 + jnp.exp(-g)) * u).astype(BF)
-        o = jnp.dot(act, wd_ref[e], preferred_element_type=F32).astype(BF).astype(F32)
-        total = total + gate * o
-    out_ref[...] = total.astype(BF)
-
-
-def run_experts(x, gates, w_gate, w_up, w_down, rows=256):
-    length, width = x.shape
-    whole = lambda a: pl.BlockSpec(a.shape, lambda i: (0,) * a.ndim, pipeline_mode=pl.Buffered(1))
-    return pl.pallas_call(
-        expert_kernel,
-        grid=(length // rows,),
-        in_specs=[
-            pl.BlockSpec((rows, width), lambda i: (i, 0)),
-            pl.BlockSpec((rows // gates.shape[2],) + gates.shape[1:], lambda i: (i, 0, 0)),
-            whole(w_gate),
-            whole(w_up),
-            whole(w_down),
-        ],
-        out_specs=pl.BlockSpec((rows, width), lambda i: (i, 0)),
-        out_shape=jax.ShapeDtypeStruct((length, width), BF),
-        compiler_params=pltpu.CompilerParams(vmem_limit_bytes=VMEM_CAP),
-        name="experts",
-    )(x, gates, w_gate, w_up, w_down)
+    )(steps, used, fill, q, near, cache, rows, w_out)
 
 
 MESH_ID = pl.DeviceIdType.MESH
@@ -346,131 +276,204 @@
     return {key: i for i, key in enumerate(keys)}
 
 
-def torus_scatter(parts, land, rows, sends, receives, keys):
-    place, head = lax.axis_index("tok"), lax.axis_index("head")
-    half_rows, part = rows // 2, rows // 4
-    started = []
-
-    def unit(half, a, b):
-        return (a, b) if half == 0 else (b, a)
-
-    def spot(key):
-        kind, half, a, sign = key
-        second = kind.endswith("2")
-        base = half * half_rows
+class TorusScatter:
+    def __init__(self, parts, land, rows, sends, receives):
+        self.parts, self.land, self.sends, self.receives = parts, land, sends, receives
+        self.keys = scatter_messages()
+        self.rows = rows
+        self.place, self.head = lax.axis_index("tok"), lax.axis_index("head")
+
+    def slot(self, half, a, b):
+        return place_of(self.place, *((a, b) if half == 0 else (b, a)))
+
+    def spot(self, kind, half, a, sign):
+        base, part = half * self.rows // 2, self.rows // 4
         low, high = pl.ds(base, part), pl.ds(base + part, part)
         with_far, plain = (low, high) if sign == 1 else (high, low)
         distance = 2 if kind.startswith("far") else sign
-        offset = (distance, 0) if second else (a, distance)
-        rows_of = plain if kind.startswith("plain") else with_far
-        return place_of(place, *unit(half, *offset)), rows_of
-
-    def copy(key):
+        offset = (distance, 0) if kind.endswith("2") else (a, distance)
+        return self.slot(half, *offset), plain if kind.startswith("plain") else with_far
+
+    def copy(self, *key):
         kind, half, a, sign = key
-        slot, rows_of = spot(key)
-        step = unit(half, sign, 0) if kind.endswith("2") else unit(half, 0, sign)
+        slot, rows_of = self.spot(*key)
+        step = (sign, 0) if kind.endswith("2") else (0, sign)
         return pltpu.make_async_remote_copy(
-            src_ref=parts.at[slot, rows_of],
-            dst_ref=land.at[keys[key]],
-            send_sem=sends.at[keys[key]],
-            recv_sem=receives.at[keys[key]],
-            device_id=(place_of(place, *step), head),
+            src_ref=self.parts.at[slot, rows_of],
+            dst_ref=self.land.at[self.keys[key]],
+            send_sem=self.sends.at[self.keys[key]],
+            recv_sem=self.receives.at[self.keys[key]],
+            device_id=(self.slot(half, *step), self.head),
             device_id_type=MESH_ID,
         )
 
-    def send(*key):
-        c = copy(key)
-        c.start()
-        started.append(c)
-
-    def add(key, slot, rows_of):
-        copy(key).wait_recv()
-        parts[slot, rows_of] = (
-            parts[slot, rows_of].astype(F32) + land[keys[key]].astype(F32)
-        ).astype(parts.dtype)
-
-    order = (2, -1, 1, 0)
-    for a in order:
+    def send(self, *key):
+        self.copy(*key).start()
+
+    def add(self, key, slot, rows_of):
+        self.copy(*key).wait_recv()
+        self.parts[slot, rows_of] = (
+            self.parts[slot, rows_of].astype(F32) + self.land[self.keys[key]].astype(F32)
+        ).astype(self.parts.dtype)
+
+    def send_unit(self, dx, dy):
+        for half, a, b in ((0, dx, dy), (1, dy, dx)):
+            if b == 2:
+                self.send("far", half, a, 1)
+                self.send("far", half, a, -1)
+            elif b != 0:
+                self.send("plain", half, a, b)
+
+    def pass_on(self, half, a):
         for sign in (1, -1):
-            for half in (0, 1):
-                send("far", half, a, sign)
+            slot, rows_of = self.spot("added", half, a, sign)
+            self.add(("far", half, a, sign), slot, rows_of)
+            self.send("added", half, a, sign)
+
+    def complete(self, half, a):
+        slot = self.slot(half, a, 0)
         for sign in (1, -1):
-            for half in (0, 1):
-                send("plain", half, a, sign)
-        yield
-    for step in range(len(order) + 1):
-        if step < len(order):
-            a = order[step]
-            for sign in (1, -1):
-                for half in (0, 1):
-                    slot, rows_of = spot(("added", half, a, sign))
-                    add(("far", half, a, sign), slot, rows_of)
-                    send("added", half, a, sign)
-            yield
-        if step > 0:
-            a = order[step - 1]
-            for half in (0, 1):
-                slot = place_of(place, *unit(half, a, 0))
-                for sign in (1, -1):
-                    for kind in ("plain", "added"):
-                        _, rows_of = spot((kind, half, a, sign))
-                        add((kind, half, a, sign), slot, rows_of)
-                if a == 2:
-                    for sign in (1, -1):
-                        send("far2", half, 0, sign)
-                elif a != 0:
-                    send("plain2", half, 0, a)
-            yield
-        if step == 3:
+            for kind in ("plain", "added"):
+                _, rows_of = self.spot(kind, half, a, sign)
+                self.add((kind, half, a, sign), slot, rows_of)
+        if a == 2:
+            self.send("far2", half, 0, 1)
+            self.send("far2", half, 0, -1)
+        elif a != 0:
+            self.send("plain2", half, 0, a)
+
+    def pass_on_last(self, half):
+        for sign in (1, -1):
+            slot, rows_of = self.spot("added2", half, 0, sign)
+            self.add(("far2", half, 0, sign), slot, rows_of)
+            self.send("added2", half, 0, sign)
+
+    def finish(self):
+        for kind in ("plain2", "added2"):
             for half in (0, 1):
                 for sign in (1, -1):
-                    slot, rows_of = spot(("added2", half, 0, sign))
-                    add(("far2", half, 0, sign), slot, rows_of)
-                    send("added2", half, 0, sign)
-            yield
+                    _, rows_of = self.spot(kind, half, 0, sign)
+                    self.add((kind, half, 0, sign), self.place, rows_of)
+
+    def drain(self):
+        for key in self.keys:
+            self.copy(*key).wait_send()
+
+
+PAIRS = (
+    ((2, 2), (2, -1)),
+    ((-1, 2), (2, 1)),
+    ((1, 2), (2, 0)),
+    ((0, 2), (-1, -1)),
+    ((1, -1), (-1, 1)),
+    ((1, 1), (-1, 0)),
+    ((0, -1), (1, 0)),
+    ((0, 1), (0, 0)),
+)
+
+
+def pair_slot(place, step, member):
+    dx, dy = 0, 0
+    for k, pair in enumerate(PAIRS):
+        dx = jnp.where(step == k, pair[member][0], dx)
+        dy = jnp.where(step == k, pair[member][1], dy)
+    return place_of(place, dx, dy)
+
+
+def experts_kernel(
+    x_ref, gates_ref, wg_ref, wu_ref, wd_ref, hidden_ref, out_ref, parts, land, held, sends, receives, load_sems
+):
+    place = lax.axis_index("tok")
+    rows = parts.shape[1]
+
+    def load(step, side, member):
+        return pltpu.make_async_copy(
+            x_ref.at[pair_slot(place, step, member)],
+            held.at[side, pl.ds(member * rows, rows)],
+            load_sems.at[side, member],
+        )
+
+    for member in (0, 1):
+        load(0, 0, member).start()
+    greet(torus_peers())
+    back = TorusScatter(parts, land, rows, sends, receives)
+
+    @pl.loop(0, len(PAIRS))
+    def _(step):
+        side = step % 2
+        for member in (0, 1):
+            load(step, side, member).wait()
+
+        @pl.when(step < len(PAIRS) - 1)
+        def _():
+            for member in (0, 1):
+                load(step + 1, 1 - side, member).start()
+
+        slots = [pair_slot(place, step, member) for member in (0, 1)]
+        gates = jnp.concatenate([gates_ref[s].T for s in slots], axis=0)
+        x = held[side]
+        total = jnp.zeros((2 * rows, wd_ref.shape[2]), F32)
+        for e in range(wg_ref.shape[0]):
+            g = jnp.dot(x, wg_ref[e], preferred_element_type=F32)
+            u = jnp.dot(x, wu_ref[e], preferred_element_type=F32)
+            act = (g / (1.0 + jnp.exp(-g)) * u).astype(BF)
+            o = jnp.dot(act, wd_ref[e], preferred_element_type=F32).astype(BF).astype(F32)
+            total = total + gates[:, e : e + 1] * o
+        for member in (0, 1):
+            parts[slots[member]] = total[member * rows : (member + 1) * rows].astype(BF)
+        for k, pair in enumerate(PAIRS):
+
+            @pl.when(step == k)
+            def _():
+                for unit in pair:
+                    back.send_unit(*unit)
+                if k == 3:
+                    for half in (0, 1):
+                        back.pass_on(half, 2)
+                if k == 5:
+                    for half in (0, 1):
+                        for a in (-1, 1):
+                            back.pass_on(half, a)
+                    for half in (0, 1):
+                        back.complete(half, 2)
+
     for half in (0, 1):
-        for sign in (1, -1):
-            for kind in ("plain2", "added2"):
-                _, rows_of = spot((kind, half, 0, sign))
-                add((kind, half, 0, sign), place, rows_of)
-    for c in started:
-        c.wait_send()
-    yield
-
-
-def scatter_kernel(x_ref, hidden_ref, out_ref, parts, land, sends, receives, own_sems):
-    keys = scatter_messages()
-    loads = [pltpu.make_async_copy(x_ref.at[s], parts.at[s], own_sems.at[s]) for s in range(parts.shape[0])]
-    for c in loads:
-        c.start()
-    greet(torus_peers())
-    for c in loads:
-        c.wait()
-    for _ in torus_scatter(parts, land, parts.shape[1], sends, receives, keys):
-        pass
-    out_ref[...] = (hidden_ref[...] + parts[lax.axis_index("tok")].astype(F32)).astype(out_ref.dtype)
-
-
-def scatter_tok(x, hidden, collective_id):
+        back.pass_on(half, 0)
+    for half in (0, 1):
+        for a in (-1, 1):
+            back.complete(half, a)
+    for half in (0, 1):
+        back.pass_on_last(half)
+    for half in (0, 1):
+        back.complete(half, 0)
+    back.finish()
+    back.drain()
+    out_ref[...] = (hidden_ref[...] + parts[place].astype(F32)).astype(out_ref.dtype)
+
+
+def run_experts(x, gates, w_gate, w_up, w_down, hidden, collective_id):
     count = len(scatter_messages())
     _, rows, width = x.shape
+    dma = pltpu.SemaphoreType.DMA
+    vmem = pl.BlockSpec(memory_space=pltpu.VMEM)
     return pl.pallas_call(
-        scatter_kernel,
-        in_specs=[pl.BlockSpec(memory_space=pl.ANY), pl.BlockSpec(memory_space=pltpu.VMEM)],
-        out_specs=pl.BlockSpec(memory_space=pltpu.VMEM),
+        experts_kernel,
+        in_specs=[pl.BlockSpec(memory_space=pl.ANY)] + [vmem] * 5,
+        out_specs=vmem,
         out_shape=jax.ShapeDtypeStruct((rows, width), x.dtype),
         scratch_shapes=[
             pltpu.VMEM(x.shape, x.dtype),
             pltpu.VMEM((count, rows // 4, width), x.dtype),
-            pltpu.SemaphoreType.DMA((count,)),
-            pltpu.SemaphoreType.DMA((count,)),
-            pltpu.SemaphoreType.DMA((16,)),
+            pltpu.VMEM((2, 2 * rows, width), x.dtype),
+            dma((count,)),
+            dma((count,)),
+            dma((2, 2)),
         ],
         compiler_params=pltpu.CompilerParams(
             collective_id=collective_id, has_side_effects=True, vmem_limit_bytes=VMEM_CAP
         ),
-        name="scatter_tok",
-    )(x, hidden)
+        name="experts",
+    )(x, gates, w_gate, w_up, w_down, hidden)
 
 
 def ring_messages(kinds):
@@ -536,17 +539,20 @@
     send("near", -1)
     send("pair", 0)
     yield
+    arrive("pair", 0)
+    yield
     for sign in (1, -1):
         arrive("near", sign)
         send("far", sign)
         send("pair", -sign)
     yield
+    for dz in (1, -1):
+        arrive("pair", dz)
+    yield
     for sign in (1, -1):
         arrive("far", sign)
         send("half", sign)
     yield
-    for dz in (0, 1, -1):
-        arrive("pair", dz)
     for sign in (1, -1):
         arrive("half", sign)
     for c in started:
@@ -554,17 +560,22 @@
     yield
 
 
-def opening_kernel(x_ref, cache_ref, gates_ref, x_out, cache_out, gates_out, ts, tr, hs, hr, gs, gr, own_sems):
+def opening_kernel(
+    x_ref, cache_ref, gates_ref, wq_ref, wkv_ref, angles_ref, q_ref, near_ref, cache_out, gates_out,
+    gathered, cos_ref, sin_ref, ts, tr, hs, hr, gs, gr, ks, kr, own_sems,
+):
     place, head = lax.axis_index("tok"), lax.axis_index("head")
     count = gates_ref.shape[0]
+    rows = x_ref.shape[0]
+    row_len = near_ref.shape[0] // 2
+    heads = q_ref.shape[0]
     others = [((place + d) % count, head) for d in range(1, count)]
     greet(others + ring_peers())
     mine = [
-        pltpu.make_async_copy(x_ref, x_out.at[head], own_sems.at[0]),
-        pltpu.make_async_copy(cache_ref, cache_out.at[place], own_sems.at[1]),
-        pltpu.make_async_copy(gates_ref.at[place], gates_out.at[place], own_sems.at[2]),
+        pltpu.make_async_copy(cache_ref, cache_out.at[place], own_sems.at[0]),
+        pltpu.make_async_copy(gates_ref.at[place], gates_out.at[place], own_sems.at[1]),
     ]
-    one = ring_gather(x_ref, x_out, x_ref.shape[0], hs, hr, GATHER_RING)
+    one = ring_gather(x_ref, gathered, rows, hs, hr, GATHER_RING)
     two = torus_gather(cache_ref, cache_out, cache_ref.shape[0], ts, tr, torus_messages())
 
     def gate_copy(d, landing=False):
@@ -579,18 +590,60 @@
             device_id_type=MESH_ID,
         )
 
+    def onward(block):
+        at = pl.multiple_of(block * rows, rows)
+        return pltpu.make_async_remote_copy(
+            src_ref=near_ref.at[pl.ds(row_len + at, rows)],
+            dst_ref=near_ref.at[pl.ds(at, rows)],
+            send_sem=ks.at[block],
+            recv_sem=kr.at[block],
+            device_id=((place + 1) % count, head),
+            device_id_type=MESH_ID,
+        )
+
+    def project(block, x):
+        at = pl.multiple_of(block * rows, rows)
+        here = pl.ds(at, rows)
+        turned = turn(x, wq_ref[...], wkv_ref[...], cos_ref[here], sin_ref[here])
+        pad = jnp.zeros((rows, HS), BF)
+        for h in range(heads):
+            q_ref[h, here] = jnp.concatenate([turned[:, h * HS : (h + 1) * HS], pad], axis=1)
+        near_ref[pl.ds(row_len + at, rows)] = turned[:, heads * HS :]
+        onward(block).start()
+
     next(one)
     next(two)
     for c in mine:
         c.start()
     for d in range(1, count):
         gate_copy(d).start()
-    for _ in range(2):
-        next(one)
-        next(two)
+    half = HS // 2
+    cos, sin = angles_ref[:half].T, angles_ref[half:].T
+    cos_ref[...] = jnp.concatenate([cos] * 4, axis=1)
+    sin_ref[...] = jnp.concatenate([sin] * 4, axis=1)
+
+    def project_slots(*slots):
+        for block in slots:
+            project(block, gathered[block])
+
+    project(head, x_ref[...])
+    next(two)
+    next(one)
+    project_slots(head_of(head, 0, 1))
+    next(two)
+    next(two)
+    next(one)
+    project_slots(head_of(head, 1), head_of(head, -1))
+    next(one)
+    project_slots(head_of(head, 1, 1), head_of(head, -1, 1))
+    next(two)
+    next(two)
+    next(one)
+    project_slots(head_of(head, 2))
+    next(two)
+    next(one)
+    project_slots(head_of(head, 2, 1))
     for _ in two:
-        pass
-    for _ in one:
         pass
     for d in range(1, count):
         gate_copy(d, True).wait_recv()
@@ -598,24 +651,50 @@
         gate_copy(d).wait_send()
     for c in mine:
         c.wait()
-
-
-def opening(x, cache, gates, collective_id):
+    for dz in range(4):
+        for flip in (0, 1):
+            onward(head_of(head, dz, flip)).wait_recv()
+    for dz in range(4):
+        for flip in (0, 1):
+            onward(head_of(head, dz, flip)).wait_send()
+
+
+def opening(x, cache, gates, w_query, w_keyval, angles, collective_id):
     t, r, n = len(torus_messages()), len(GATHER_RING), gates.shape[0]
+    rows, width = x.shape
+    length = angles.shape[1]
+    heads = w_query.shape[0] // HS
     dma = pltpu.SemaphoreType.DMA
+    vmem, anywhere = pl.BlockSpec(memory_space=pltpu.VMEM), pl.BlockSpec(memory_space=pl.ANY)
     return pl.pallas_call(
         opening_kernel,
-        in_specs=[pl.BlockSpec(memory_space=pltpu.VMEM)] * 3,
-        out_specs=[pl.BlockSpec(memory_space=pl.ANY)] * 3,
+        in_specs=[vmem] * 6,
+        out_specs=[vmem, vmem, anywhere, anywhere],
         out_shape=[
-            jax.ShapeDtypeStruct((8,) + x.shape, x.dtype),
+            jax.ShapeDtypeStruct((heads, length, 128), BF),
+            jax.ShapeDtypeStruct((2 * length, 128), BF),
             jax.ShapeDtypeStruct((n,) + cache.shape, cache.dtype),
             jax.ShapeDtypeStruct(gates.shape, gates.dtype),
         ],
-        scratch_shapes=[dma((t,)), dma((t,)), dma((r,)), dma((r,)), dma((n,)), dma((n,)), dma((3,))],
-        compiler_params=pltpu.CompilerParams(collective_id=collective_id, has_side_effects=True),
+        scratch_shapes=[
+            pltpu.VMEM((length // rows, rows, width), BF),
+            pltpu.VMEM((length, 128), F32),
+            pltpu.VMEM((length, 128), F32),
+            dma((t,)),
+            dma((t,)),
+            dma((r,)),
+            dma((r,)),
+            dma((n,)),
+            dma((n,)),
+            dma((length // rows,)),
+            dma((length // rows,)),
+            dma((2,)),
+        ],
+        compiler_params=pltpu.CompilerParams(
+            collective_id=collective_id, has_side_effects=True, vmem_limit_bytes=VMEM_CAP
+        ),
         name="opening",
-    )(x, cache, gates)
+    )(x, cache, gates, w_query, w_keyval, angles)
 
 
 def ring_scatter(parts, pair_land, land, rows, sends, receives, keys):
@@ -771,21 +850,18 @@
     gates = jnp.sum(jnp.where(routes.T[None] == experts, route_gates.T[None], 0.0), axis=1)
     gates = gates.reshape(tok_count, exp_local, -1)
     gates = jnp.concatenate([gates, jnp.zeros((tok_count, 8 - exp_local, gates.shape[2]), F32)], axis=1)
-    gathered, cache, gates_all = opening(normed, prefix_cache, gates, 1)
-    gathered = gathered.reshape(row_len, -1)
-    cache = cache.reshape(-1, cache.shape[-1])
 
     padded = jnp.concatenate([jnp.full((row_len,), -1, jnp.int32), segments])
     window = lax.dynamic_slice_in_dim(padded, place * row_len, 2 * row_len, 0)
     own = window[row_len:]
     begins, slabs, fills = request_tables(window, own, group_ids, prefix_owner, slab_fill)
     positions = fills + row_len + jnp.arange(row_len, dtype=jnp.int32) - begins
-    lane = jnp.arange(128, dtype=jnp.int32)
-    steps_idx = (lane % (HS // 2)).astype(F32)
+    steps_idx = jnp.arange(HS // 2, dtype=F32)
     inverse = jnp.exp(steps_idx * (-2.0 * jnp.log(10000.0) / HS))
-    angles = positions.astype(F32)[:, None] * inverse[None, :]
-    cos = jnp.cos(angles)
-    sin = jnp.where(lane % HS < HS // 2, -jnp.sin(angles), jnp.sin(angles))
+    angles = inverse[:, None] * positions.astype(F32)[None, :]
+    turns = jnp.concatenate([jnp.cos(angles), jnp.sin(angles)], axis=0)
+    q, near, cache, gates_all = opening(normed, prefix_cache, gates, w_query.T, w_keyval, turns, 1)
+    cache = cache.reshape(-1, cache.shape[-1])
 
     span = 128
     blocks = row_len // span
@@ -800,12 +876,9 @@
     used = jnp.concatenate([jnp.sum(present, axis=1, keepdims=True), used], axis=1)
     rows = jnp.concatenate([begins[None], slabs[None], jnp.zeros((6, row_len), jnp.int32)], axis=0)
 
-    q, kv_now = project(gathered, w_query, w_keyval, cos, sin)
-    kv_prev = lax.ppermute(kv_now, "tok", [(i, i + 1) for i in range(tok_count - 1)])
-    partial = attend(q, kv_prev, kv_now, cache, rows, steps, used, slab_fill, w_out)
+    partial = attend(q, near, cache, rows, steps, used, slab_fill, w_out)
     hidden, arrived = settle(partial, tokens, ffn_gain[None], 2)
-    answered = run_experts(arrived.reshape(-1, arrived.shape[-1]), gates_all, w_gate, w_up, w_down)
-    return scatter_tok(answered.reshape(arrived.shape), hidden, 3)
+    return run_experts(arrived, gates_all, w_gate, w_up, w_down, hidden, 3)
 
 
 def solution(mesh):

time: 218 us -> 180 us (0.83)
  Pallas kernels: 195 us -> 165 us
  starting transfers between devices: 2.78 us -> 0 us
  local copies, waits for them, and re-layouts: 7.61 us -> 5.34 us
    pallas_call x4 -> x2, Pallas kernels: 109 us -> 78.5 us  [the longest x1 45.2 us: run_experts(): pl.pallas_call(experts_kernel, in_specs=[pl.BlockSpec(memory_space=pl.ANY...]
    select_n x1 -> x0, other arithmetic: 3.08 us -> none  [local(): sin = jnp.where(lane % HS < HS // 2, -jnp.sin(angles), jnp.sin(angles))]
    unnamed x6 -> x1, local copies, waits for them, and re-layouts: 4.72 us -> 1.77 us
    ppermute x1 -> x0, starting transfers between devices: 2.78 us -> none  [local(): lax.ppermute(kv_now, 'tok', [(i, i + 1) for i in range(tok_count - 1)])]
  transfers between devices with their start and end apart: 1 -> 0, of which waited for: 1 -> 0; matrix products, arithmetic and copies ran while one was open for 2% -> 0% of each run, Pallas kernels for 0% -> 0%
where the time goes in v3:
time: 180 us
  Pallas kernels  165 us (92%)
  other arithmetic  9.59 us (5%)
  local copies, waits for them, and re-layouts  5.34 us (3%)
    pallas_call x1, Pallas kernels, settle(): pl.pallas_call(settle_kernel, in_specs=[pl.BlockSpec(memory_space=pl.ANY)...  64.5 us
    pallas_call x1, Pallas kernels, run_experts(): pl.pallas_call(experts_kernel, in_specs=[pl.BlockSpec(memory_space=pl.ANY...  45.2 us
    pallas_call x1, Pallas kernels, opening(): pl.pallas_call(opening_kernel, in_specs=[vmem] * 6, out_specs=[vmem, vmem...  33.2 us
    pallas_call x1, Pallas kernels, attend(): pl.pallas_call(attend_kernel, grid_spec=pltpu.PrefetchScalarGridSpec(num_...  21.6 us

profile of v3, /device:TPU:0, one launch (start us, length us, event | category | flops | bytes accessed | tf_op | source)
XLA Modules:
  0.0 179.6 jit_solution(14178603050490065452)
XLA Ops:
  0.0 0.8 select_reduce_fusion.5
  0.8 0.7 select_reduce_fusion.4
  1.5 1.2 fusion
  2.7 0.1 pad.4.clone
  2.8 0.7 pad_dynamic-slice_fusion
  3.5 1.3 broadcast_in_dim.107.gain_ref
  4.8 0.7 pad_dynamic-slice_fusion.1
  5.5 0.2 convert_reduce_fusion
  5.7 0.1 select_reduce_fusion
  5.8 0.1 and_select_fusion.2
  5.9 0.2 convert_reduce_fusion.1
  6.1 0.1 reduce_sum.90
  6.2 0.1 slice_reduce_fusion
  6.3 0.6 and_select_fusion.3.steps_ref
  7.0 0.1 select_reduce_fusion.3
  7.1 0.2 select_reduce_fusion.2
  7.3 0.1 copy.21
  7.3 0.7 pad_add_fusion.used_ref
  8.0 0.7 select_reduce_fusion.1
  8.8 0.7 add_add_fusion.rows_ref
  9.4 0.6 concatenate.17.gates_ref
  10.1 0.5 multiply_cosine_fusion
  10.6 0.7 pad_maximum_fusion.angles_ref
  11.3 1.9 %fusion.2.x_ref = bf16[128,1536]{1,0:T(8,128)(2,1)} fusion(bf16[128,1536]{1,0:T(8,128)(2,1)} %tokens_ref.1, f32[1536]{0:T(1024)} %param.22, f32[128]{0:T(128)S(1)} %add_rsqrt_fusion), kind=kLoop, calls=%fused_computation.6 | loop fusion | flops 786432 | bytes 793088 | tf_op jit(solution)/shard_map/convert_element_type | solution.py:847
  13.2 33.2 %opening.1 = (bf16[3,1024,128]{2,1,0:T(8,128)(2,1)}, bf16[2048,128]{1,0:T(8,128)(2,1)}, bf16[16,512,128]{2,1,0:T(8,128)(2,1)}, f32[16,8,128]{2,1,0:T(8,128)}) custom-call(bf16[128,1536]{1,0:T(8,128)(2,1)} %fusion.2.x_ref, bf16[512,128]{1,0:T(8,128)(2,1)} %cache_ref.1, f32[16,8,128]{2,1,0:T(8,128)} %concatenate.17.gates_ref, bf16[192,1536]{1,0:T(8,128)(2,1)} %bitcast.28, ...), custom_call_target="tpu_custom_call" | custom-call | tf_op jit(solution)/shard_map/opening/pallas_call | solution.py:669
  46.5 21.6 %attend.1.part_ref = bf16[1024,1536]{1,0:T(8,128)(2,1)} custom-call(s32[8]{0:T(128)} %and_select_fusion.3.steps_ref, s32[8,17]{1,0:T(8,128)} %pad_add_fusion.used_ref, s32[16]{0:T(128)} %fill_ref.1, bf16[3,1024,128]{2,1,0:T(8,128)(2,1)} %get-tuple-element.11.q_ref, bf16[2048,128]{1,0:T(8,128)(2,1)} %get-tuple-element.12.near_ref, ...), custom_call_target="tpu_custom_call" | custom-call | tf_op jit(solution)/shard_map/attend/pallas_call | solution.py:127
  68.1 64.5 %settle.1 = (f32[128,1536]{1,0:T(8,128)}, bf16[16,128,1536]{2,1,0:T(8,128)(2,1)}) custom-call(bf16[1024,1536]{1,0:T(8,128)(2,1)} %attend.1.part_ref, bf16[128,1536]{1,0:T(8,128)(2,1)} %tokens_ref.1, f32[1,1536]{1,0:T(1,128)} %broadcast_in_dim.107.gain_ref), custom_call_target="tpu_custom_call" | custom-call | tf_op jit(solution)/shard_map/settle/pallas_call | solution.py:795
  132.7 45.2 %experts.1 = bf16[128,1536]{1,0:T(8,128)(2,1)} custom-call(bf16[16,128,1536]{2,1,0:T(8,128)(2,1)} %get-tuple-element.14.x_ref, f32[16,8,128]{2,1,0:T(8,128)} %get-tuple-element.15.gates_ref, bf16[2,1536,512]{2,1,0:T(8,128)(2,1)} %wg_ref.1, bf16[2,1536,512]{2,1,0:T(8,128)(2,1)} %wu_ref.1, bf16[2,512,1536]{2,1,0:T(8,128)(2,1)} %wd_ref.1, ...), custom_call_target="tpu_custom_call" | custom-call | tf_op jit(solution)/shard_map/experts/pallas_call | solution.py:459
  177.9 1.8 copy.23
  (8 shorter events, 0.1 us)

commit v4 on v3

--- a/solution.py
+++ b/solution.py
@@ -381,7 +381,8 @@
 
 
 def experts_kernel(
-    x_ref, gates_ref, wg_ref, wu_ref, wd_ref, hidden_ref, out_ref, parts, land, held, sends, receives, load_sems
+    x_ref, gates_ref, wg_hbm, wu_hbm, wd_hbm, hidden_ref, out_ref, parts, land, held, wg_ref, wu_ref, wd_ref,
+    sends, receives, load_sems, weight_sems,
 ):
     place = lax.axis_index("tok")
     rows = parts.shape[1]
@@ -393,8 +394,15 @@
             load_sems.at[side, member],
         )
 
+    def weight(kind, e):
+        src, dst = ((wg_hbm, wg_ref), (wu_hbm, wu_ref), (wd_hbm, wd_ref))[kind]
+        return pltpu.make_async_copy(src.at[e], dst.at[e], weight_sems.at[kind, e])
+
     for member in (0, 1):
         load(0, 0, member).start()
+    for e in range(wg_ref.shape[0]):
+        for kind in range(3):
+            weight(kind, e).start()
     greet(torus_peers())
     back = TorusScatter(parts, land, rows, sends, receives)
 
@@ -414,6 +422,12 @@
         x = held[side]
         total = jnp.zeros((2 * rows, wd_ref.shape[2]), F32)
         for e in range(wg_ref.shape[0]):
+
+            @pl.when(step == 0)
+            def _():
+                for kind in range(3):
+                    weight(kind, e).wait()
+
             g = jnp.dot(x, wg_ref[e], preferred_element_type=F32)
             u = jnp.dot(x, wu_ref[e], preferred_element_type=F32)
             act = (g / (1.0 + jnp.exp(-g)) * u).astype(BF)
@@ -455,19 +469,23 @@
     count = len(scatter_messages())
     _, rows, width = x.shape
     dma = pltpu.SemaphoreType.DMA
-    vmem = pl.BlockSpec(memory_space=pltpu.VMEM)
+    vmem, anywhere = pl.BlockSpec(memory_space=pltpu.VMEM), pl.BlockSpec(memory_space=pl.ANY)
     return pl.pallas_call(
         experts_kernel,
-        in_specs=[pl.BlockSpec(memory_space=pl.ANY)] + [vmem] * 5,
+        in_specs=[anywhere, vmem] + [anywhere] * 3 + [vmem],
         out_specs=vmem,
         out_shape=jax.ShapeDtypeStruct((rows, width), x.dtype),
         scratch_shapes=[
             pltpu.VMEM(x.shape, x.dtype),
             pltpu.VMEM((count, rows // 4, width), x.dtype),
             pltpu.VMEM((2, 2 * rows, width), x.dtype),
+            pltpu.VMEM(w_gate.shape, w_gate.dtype),
+            pltpu.VMEM(w_up.shape, w_up.dtype),
+            pltpu.VMEM(w_down.shape, w_down.dtype),
             dma((count,)),
             dma((count,)),
             dma((2, 2)),
+            dma((3, w_gate.shape[0])),
         ],
         compiler_params=pltpu.CompilerParams(
             collective_id=collective_id, has_side_effects=True, vmem_limit_bytes=VMEM_CAP
@@ -481,7 +499,7 @@
 
 
 GATHER_RING = ring_messages(
-    [("near", 1), ("near", -1), ("far", 1), ("far", -1), ("pair", 0), ("pair", 1), ("pair", -1), ("half", 1), ("half", -1)]
+    [("near", 1), ("near", -1), ("rest", 1), ("rest", -1), ("far", 1), ("far", -1), ("pair", 0), ("pair", 1), ("pair", -1), ("half", 1), ("half", -1)]
 )
 SCATTER_RING = ring_messages(
     [("pair", 2), ("pair", 1), ("pair", -1), ("pair", 0)]
@@ -506,10 +524,10 @@
     def copy(key, landing=False):
         kind, value = key
         begin, size = 0, rows
-        if kind in ("far", "half"):
+        if kind in ("near", "rest", "far", "half"):
             size = rows // 2
-            begin = 0 if value == 1 else size
-        dz = {"near": 0, "far": -value, "pair": value, "half": 2}[kind]
+            begin = size if (value == 1) == (kind == "rest") else 0
+        dz = {"near": 0, "rest": 0, "far": -value, "pair": value, "half": 2}[kind]
         crossing = kind in ("pair", "half")
         if landing:
             slot = head_of(head, dz, 1) if crossing else head_of(head, dz - value)
@@ -535,8 +553,9 @@
     def arrive(*key):
         copy(key, landing=True).wait_recv()
 
-    send("near", 1)
-    send("near", -1)
+    for kind in ("near", "rest"):
+        send(kind, 1)
+        send(kind, -1)
     send("pair", 0)
     yield
     arrive("pair", 0)
@@ -544,6 +563,8 @@
     for sign in (1, -1):
         arrive("near", sign)
         send("far", sign)
+    for sign in (1, -1):
+        arrive("rest", sign)
         send("pair", -sign)
     yield
     for dz in (1, -1):
@@ -561,8 +582,8 @@
 
 
 def opening_kernel(
-    x_ref, cache_ref, gates_ref, wq_ref, wkv_ref, angles_ref, q_ref, near_ref, cache_out, gates_out,
-    gathered, cos_ref, sin_ref, ts, tr, hs, hr, gs, gr, ks, kr, own_sems,
+    tokens_ref, gain_ref, cache_ref, gates_ref, wq_ref, wkv_ref, angles_ref, q_ref, near_ref, cache_out, gates_out,
+    x_ref, gathered, cos_ref, sin_ref, ts, tr, hs, hr, gs, gr, ks, kr, own_sems,
 ):
     place, head = lax.axis_index("tok"), lax.axis_index("head")
     count = gates_ref.shape[0]
@@ -570,6 +591,7 @@
     row_len = near_ref.shape[0] // 2
     heads = q_ref.shape[0]
     others = [((place + d) % count, head) for d in range(1, count)]
+    x_ref[...] = rms_scale(tokens_ref[...], gain_ref[...].reshape(1, -1)).astype(x_ref.dtype)
     greet(others + ring_peers())
     mine = [
         pltpu.make_async_copy(cache_ref, cache_out.at[place], own_sems.at[0]),
@@ -659,7 +681,7 @@
             onward(head_of(head, dz, flip)).wait_send()
 
 
-def opening(x, cache, gates, w_query, w_keyval, angles, collective_id):
+def opening(x, gain, cache, gates, w_query, w_keyval, angles, collective_id):
     t, r, n = len(torus_messages()), len(GATHER_RING), gates.shape[0]
     rows, width = x.shape
     length = angles.shape[1]
@@ -668,7 +690,7 @@
     vmem, anywhere = pl.BlockSpec(memory_space=pltpu.VMEM), pl.BlockSpec(memory_space=pl.ANY)
     return pl.pallas_call(
         opening_kernel,
-        in_specs=[vmem] * 6,
+        in_specs=[vmem] * 7,
         out_specs=[vmem, vmem, anywhere, anywhere],
         out_shape=[
             jax.ShapeDtypeStruct((heads, length, 128), BF),
@@ -677,6 +699,7 @@
             jax.ShapeDtypeStruct(gates.shape, gates.dtype),
         ],
         scratch_shapes=[
+            pltpu.VMEM((rows, width), BF),
             pltpu.VMEM((length // rows, rows, width), BF),
             pltpu.VMEM((length, 128), F32),
             pltpu.VMEM((length, 128), F32),
@@ -694,7 +717,7 @@
             collective_id=collective_id, has_side_effects=True, vmem_limit_bytes=VMEM_CAP
         ),
         name="opening",
-    )(x, cache, gates, w_query, w_keyval, angles)
+    )(x, gain, cache, gates, w_query, w_keyval, angles)
 
 
 def ring_scatter(parts, pair_land, land, rows, sends, receives, keys):
@@ -780,7 +803,7 @@
     ring_scatter(parts, pair_land, land, rows, rs, rr, SCATTER_RING)
     hidden = tokens_ref[...].astype(F32) + parts[head].astype(F32)
     hidden_ref[...] = hidden
-    normed[...] = rms_scale(hidden, gain_ref[...]).astype(normed.dtype)
+    normed[...] = rms_scale(hidden, gain_ref[...].reshape(1, -1)).astype(normed.dtype)
     mine = pltpu.make_async_copy(normed, out_ref.at[place], own_sems.at[8])
     mine.start()
     for _ in torus_gather(normed, out_ref, rows, ts, tr, torus_messages()):
@@ -844,7 +867,6 @@
     head_count = lax.axis_size("head")
     place = lax.axis_index("tok")
     row_len = tokens.shape[0] * head_count
-    normed = rms_scale(tokens, attn_gain).astype(BF)
     exp_local = w_gate.shape[0]
     experts = jnp.arange(EXPERTS, dtype=jnp.int32)[:, None, None]
     gates = jnp.sum(jnp.where(routes.T[None] == experts, route_gates.T[None], 0.0), axis=1)
@@ -860,7 +882,7 @@
     inverse = jnp.exp(steps_idx * (-2.0 * jnp.log(10000.0) / HS))
     angles = inverse[:, None] * positions.astype(F32)[None, :]
     turns = jnp.concatenate([jnp.cos(angles), jnp.sin(angles)], axis=0)
-    q, near, cache, gates_all = opening(normed, prefix_cache, gates, w_query.T, w_keyval, turns, 1)
+    q, near, cache, gates_all = opening(tokens, attn_gain, prefix_cache, gates, w_query.T, w_keyval, turns, 1)
     cache = cache.reshape(-1, cache.shape[-1])
 
     span = 128
@@ -877,7 +899,7 @@
     rows = jnp.concatenate([begins[None], slabs[None], jnp.zeros((6, row_len), jnp.int32)], axis=0)
 
     partial = attend(q, near, cache, rows, steps, used, slab_fill, w_out)
-    hidden, arrived = settle(partial, tokens, ffn_gain[None], 2)
+    hidden, arrived = settle(partial, tokens, ffn_gain, 2)
     return run_experts(arrived, gates_all, w_gate, w_up, w_down, hidden, 3)
 
 

time: 180 us -> 173 us (0.961)
  Pallas kernels: 165 us -> 161 us
  other arithmetic: 9.59 us -> 6.52 us
    pallas_call x1, Pallas kernels: 64.5 us -> 60.8 us  [settle(): pl.pallas_call(settle_kernel, in_specs=[pl.BlockSpec(memory_space=pl.ANY)...]
    convert_element_type x1 -> x0, other arithmetic: 1.9 us -> none  [local(): normed = rms_scale(tokens, attn_gain).astype(BF)]
where the time goes in v4:
time: 173 us; the launch traced here: 172 us
  Pallas kernels  161 us (93%)
  other arithmetic  6.52 us (4%)
  local copies, waits for them, and re-layouts  4.06 us (2%)
    pallas_call x1, Pallas kernels, settle(): pl.pallas_call(settle_kernel, in_specs=[pl.BlockSpec(memory_space=pl.ANY)...  60.8 us
    pallas_call x1, Pallas kernels, run_experts(): pl.pallas_call(experts_kernel, in_specs=[anywhere, vmem] + [anywhere] * 3...  45 us
    pallas_call x1, Pallas kernels, opening(): pl.pallas_call(opening_kernel, in_specs=[vmem] * 7, out_specs=[vmem, vmem...  33.5 us
    pallas_call x1, Pallas kernels, attend(): pl.pallas_call(attend_kernel, grid_spec=pltpu.PrefetchScalarGridSpec(num_...  21.9 us

profile of v4, /device:TPU:0, one launch (start us, length us, event | category | flops | bytes accessed | tf_op | source)
XLA Modules:
  0.0 171.9 jit_solution(9991196874021901349)
XLA Ops:
  0.0 0.8 select_reduce_fusion.5
  0.8 0.7 select_reduce_fusion.4
  1.5 0.1 pad.4.clone
  1.6 0.7 pad_dynamic-slice_fusion
  2.3 0.7 pad_dynamic-slice_fusion.1
  3.0 0.2 convert_reduce_fusion
  3.2 0.1 select_reduce_fusion
  3.4 0.1 and_select_fusion.2
  3.4 0.2 convert_reduce_fusion.1
  3.7 0.1 reduce_sum.81
  3.8 0.1 slice_reduce_fusion
  3.9 0.6 and_select_fusion.3.steps_ref
  4.5 0.1 select_reduce_fusion.3
  4.6 0.2 select_reduce_fusion.2
  4.8 0.1 copy.21
  4.9 0.7 pad_add_fusion.used_ref
  5.6 0.7 select_reduce_fusion.1
  6.3 0.7 add_add_fusion.rows_ref
  7.0 0.6 concatenate.17.gates_ref
  7.6 0.5 multiply_cosine_fusion
  8.1 0.7 pad_maximum_fusion.angles_ref
  8.9 33.5 %opening.1 = (bf16[3,1024,128]{2,1,0:T(8,128)(2,1)}, bf16[2048,128]{1,0:T(8,128)(2,1)}, bf16[16,512,128]{2,1,0:T(8,128)(2,1)}, f32[16,8,128]{2,1,0:T(8,128)}) custom-call(bf16[128,1536]{1,0:T(8,128)(2,1)} %tokens_ref.3, f32[1536]{0:T(1024)} %gain_ref.2, bf16[512,128]{1,0:T(8,128)(2,1)} %cache_ref.1, f32[16,8,128]{2,1,0:T(8,128)} %concatenate.17.gates_ref, ...), custom_call_target="tpu_custom_call" | custom-call | tf_op jit(solution)/shard_map/opening/pallas_call | solution.py:691
  42.4 21.9 %attend.1.part_ref = bf16[1024,1536]{1,0:T(8,128)(2,1)} custom-call(s32[8]{0:T(128)} %and_select_fusion.3.steps_ref, s32[8,17]{1,0:T(8,128)} %pad_add_fusion.used_ref, s32[16]{0:T(128)} %fill_ref.1, bf16[3,1024,128]{2,1,0:T(8,128)(2,1)} %get-tuple-element.11.q_ref, bf16[2048,128]{1,0:T(8,128)(2,1)} %get-tuple-element.12.near_ref, ...), custom_call_target="tpu_custom_call" | custom-call | tf_op jit(solution)/shard_map/attend/pallas_call | solution.py:127
  64.2 60.8 %settle.1 = (f32[128,1536]{1,0:T(8,128)}, bf16[16,128,1536]{2,1,0:T(8,128)(2,1)}) custom-call(bf16[1024,1536]{1,0:T(8,128)(2,1)} %attend.1.part_ref, bf16[128,1536]{1,0:T(8,128)(2,1)} %tokens_ref.3, f32[1536]{0:T(1024)} %gain_ref.3), custom_call_target="tpu_custom_call" | custom-call | tf_op jit(solution)/shard_map/settle/pallas_call | solution.py:818
  125.1 45.0 %experts.1 = bf16[128,1536]{1,0:T(8,128)(2,1)} custom-call(bf16[16,128,1536]{2,1,0:T(8,128)(2,1)} %get-tuple-element.14.x_ref, f32[16,8,128]{2,1,0:T(8,128)} %get-tuple-element.15.gates_ref, bf16[2,1536,512]{2,1,0:T(8,128)(2,1)} %wg_hbm.1, bf16[2,1536,512]{2,1,0:T(8,128)(2,1)} %wu_hbm.1, bf16[2,512,1536]{2,1,0:T(8,128)(2,1)} %wd_hbm.1, ...), custom_call_target="tpu_custom_call" | custom-call | tf_op jit(solution)/shard_map/experts/pallas_call | solution.py:473
  170.1 1.8 %copy.23 = bf16[128,1536]{1,0:T(8,128)(2,1)} copy(bf16[128,1536]{1,0:T(8,128)(2,1)} %experts.1) | data formatting | bytes 786432
  (7 shorter events, 0.1 us)

commit v5 on v4

--- a/solution.py
+++ b/solution.py
@@ -75,47 +75,55 @@
     def scores(kv):
         return lax.dot_general(kv, queries, (((1,), (1,)), ((), ())), preferred_element_type=F32)
 
-    def absorb(s, kv, carry):
+    def absorb(blocks, carry):
         peak, total, acc = carry
-        peak_new = jnp.maximum(peak, jnp.max(s, axis=0, keepdims=True))
+        peak_new = peak
+        for s, _ in blocks:
+            peak_new = jnp.maximum(peak_new, jnp.max(s, axis=0, keepdims=True))
         factor = jnp.exp2((peak - peak_new) * scale)
-        weights = jnp.exp2((s - peak_new) * scale)
-        total = total * factor + jnp.sum(weights, axis=0, keepdims=True)
-        values = kv.T[HS:]
-        acc = acc * factor + jnp.dot(values, weights.astype(BF), preferred_element_type=F32)
+        total, acc = total * factor, acc * factor
+        for s, kv in blocks:
+            weights = jnp.exp2((s - peak_new) * scale)
+            total = total + jnp.sum(weights, axis=0, keepdims=True)
+            acc = acc + jnp.dot(kv.T[HS:], weights.astype(BF), preferred_element_type=F32)
         return peak_new, total, acc
 
-    kv = near_ref[pl.ds(pl.multiple_of(offset, span), span)]
-    key = lax.broadcasted_iota(jnp.int32, (span, wide), 0)
-    query = lax.broadcasted_iota(jnp.int32, (span, wide), 1) % span
-    s = jnp.where((key <= query) & (key >= begins - offset), scores(kv), NEG_FILL)
+    def own():
+        kv = near_ref[pl.ds(pl.multiple_of(offset, span), span)]
+        key = lax.broadcasted_iota(jnp.int32, (span, wide), 0)
+        query = lax.broadcasted_iota(jnp.int32, (span, wide), 1) % span
+        return jnp.where((key <= query) & (key >= begins - offset), scores(kv), NEG_FILL), kv
+
+    chunk = 2 * span
+
+    def near(step):
+        first = pl.multiple_of(offset - (step + 1) * chunk, span)
+        kv = near_ref[pl.ds(first, chunk)]
+        key = lax.broadcasted_iota(jnp.int32, (chunk, wide), 0)
+        return jnp.where(key >= begins - first, scores(kv), NEG_FILL), kv
+
+    def far(step):
+        slab = used_ref[block, step + 1]
+        kv = cache_ref[pl.ds(pl.multiple_of(slab * PREFIX, PREFIX), PREFIX)]
+        key = lax.broadcasted_iota(jnp.int32, (PREFIX, wide), 0)
+        limit = jnp.where(slabs == slab, fill_ref[slab], 0)
+        return jnp.where(key < limit, scores(kv), NEG_FILL), kv
+
+    def sweep(piece, start, count, carry):
+        pairs = count // 2
+        carry = lax.fori_loop(
+            0, pairs, lambda i, c: absorb([piece(start + 2 * i), piece(start + 2 * i + 1)], c), carry
+        )
+        return lax.fori_loop(2 * pairs, count, lambda i, c: absorb([piece(start + i)], c), carry)
+
     carry = (
         jnp.full((1, wide), NEG_FILL, F32),
         jnp.zeros((1, wide), F32),
         jnp.zeros((HS, wide), F32),
     )
-    carry = absorb(s, kv, carry)
-
-    chunk = 2 * span
-
-    def near_step(step, carry):
-        first = pl.multiple_of(offset - (step + 1) * chunk, span)
-        kv = near_ref[pl.ds(first, chunk)]
-        key = lax.broadcasted_iota(jnp.int32, (chunk, wide), 0)
-        s = jnp.where(key >= begins - first, scores(kv), NEG_FILL)
-        return absorb(s, kv, carry)
-
-    carry = lax.fori_loop(0, steps_ref[block], near_step, carry)
-
-    def far_step(step, carry):
-        slab = used_ref[block, step + 1]
-        kv = cache_ref[pl.ds(pl.multiple_of(slab * PREFIX, PREFIX), PREFIX)]
-        key = lax.broadcasted_iota(jnp.int32, (PREFIX, wide), 0)
-        limit = jnp.where(slabs == slab, fill_ref[slab], 0)
-        s = jnp.where(key < limit, scores(kv), NEG_FILL)
-        return absorb(s, kv, carry)
-
-    _, total, acc = lax.fori_loop(0, used_ref[block, 0], far_step, carry)
+    carry = absorb([own(), far(0)], carry)
+    carry = sweep(near, 0, steps_ref[block], carry)
+    _, total, acc = sweep(far, 1, used_ref[block, 0] - 1, carry)
     mixed = (acc / total).T
     mixed = jnp.concatenate([mixed[h * span : (h + 1) * span] for h in range(heads)], axis=1)
     out_ref[...] = jnp.dot(mixed.astype(BF), wout_ref[...], preferred_element_type=F32).astype(BF)

time: 173 us -> 169 us (0.977)
  Pallas kernels: 161 us -> 158 us
    pallas_call x1, Pallas kernels: 60.8 us -> 58.3 us  [settle(): pl.pallas_call(settle_kernel, in_specs=[pl.BlockSpec(memory_space=pl.ANY)...]
    pallas_call x1, Pallas kernels: 21.9 us -> 19.9 us  [attend(): pl.pallas_call(attend_kernel, grid_spec=pltpu.PrefetchScalarGridSpec(num_...]
where the time goes in v5:
time: 169 us; the launch traced here: 168 us
  Pallas kernels  158 us (93%)
  other arithmetic  6.52 us (4%)
  local copies, waits for them, and re-layouts  4.06 us (2%)
    pallas_call x1, Pallas kernels, settle(): pl.pallas_call(settle_kernel, in_specs=[pl.BlockSpec(memory_space=pl.ANY)...  58.3 us
    pallas_call x1, Pallas kernels, run_experts(): pl.pallas_call(experts_kernel, in_specs=[anywhere, vmem] + [anywhere] * 3...  46.1 us
    pallas_call x1, Pallas kernels, opening(): pl.pallas_call(opening_kernel, in_specs=[vmem] * 7, out_specs=[vmem, vmem...  33.5 us
    pallas_call x1, Pallas kernels, attend(): pl.pallas_call(attend_kernel, grid_spec=pltpu.PrefetchScalarGridSpec(num_...  19.9 us

profile of v5, /device:TPU:0, one launch (start us, length us, event | category | flops | bytes accessed | tf_op | source)
XLA Modules:
  0.0 168.5 jit_solution(1032535980488150568)
XLA Ops:
  0.0 0.8 select_reduce_fusion.5
  0.8 0.7 select_reduce_fusion.4
  1.5 0.1 pad.4.clone
  1.6 0.7 pad_dynamic-slice_fusion
  2.3 0.7 pad_dynamic-slice_fusion.1
  3.0 0.2 convert_reduce_fusion
  3.2 0.1 select_reduce_fusion
  3.4 0.1 and_select_fusion.2
  3.4 0.2 convert_reduce_fusion.1
  3.7 0.1 reduce_sum.81
  3.8 0.1 slice_reduce_fusion
  3.9 0.6 and_select_fusion.3.steps_ref
  4.5 0.1 select_reduce_fusion.3
  4.6 0.2 select_reduce_fusion.2
  4.8 0.1 copy.21
  4.9 0.7 pad_add_fusion.used_ref
  5.6 0.7 select_reduce_fusion.1
  6.3 0.7 add_add_fusion.rows_ref
  7.0 0.6 concatenate.17.gates_ref
  7.6 0.5 multiply_cosine_fusion
  8.1 0.7 pad_maximum_fusion.angles_ref
  8.9 33.5 %opening.1 = (bf16[3,1024,128]{2,1,0:T(8,128)(2,1)}, bf16[2048,128]{1,0:T(8,128)(2,1)}, bf16[16,512,128]{2,1,0:T(8,128)(2,1)}, f32[16,8,128]{2,1,0:T(8,128)}) custom-call(bf16[128,1536]{1,0:T(8,128)(2,1)} %tokens_ref.3, f32[1536]{0:T(1024)} %gain_ref.2, bf16[512,128]{1,0:T(8,128)(2,1)} %cache_ref.1, f32[16,8,128]{2,1,0:T(8,128)} %concatenate.17.gates_ref, ...), custom_call_target="tpu_custom_call" | custom-call | tf_op jit(solution)/shard_map/opening/pallas_call | solution.py:699
  42.4 19.9 %attend.1.part_ref = bf16[1024,1536]{1,0:T(8,128)(2,1)} custom-call(s32[8]{0:T(128)} %and_select_fusion.3.steps_ref, s32[8,17]{1,0:T(8,128)} %pad_add_fusion.used_ref, s32[16]{0:T(128)} %fill_ref.1, bf16[3,1024,128]{2,1,0:T(8,128)(2,1)} %get-tuple-element.11.q_ref, bf16[2048,128]{1,0:T(8,128)(2,1)} %get-tuple-element.12.near_ref, ...), custom_call_target="tpu_custom_call" | custom-call | tf_op jit(solution)/shard_map/attend/pallas_call | solution.py:135
  62.3 58.3 %settle.1 = (f32[128,1536]{1,0:T(8,128)}, bf16[16,128,1536]{2,1,0:T(8,128)(2,1)}) custom-call(bf16[1024,1536]{1,0:T(8,128)(2,1)} %attend.1.part_ref, bf16[128,1536]{1,0:T(8,128)(2,1)} %tokens_ref.3, f32[1536]{0:T(1024)} %gain_ref.3), custom_call_target="tpu_custom_call" | custom-call | tf_op jit(solution)/shard_map/settle/pallas_call | solution.py:826
  120.6 46.1 %experts.1 = bf16[128,1536]{1,0:T(8,128)(2,1)} custom-call(bf16[16,128,1536]{2,1,0:T(8,128)(2,1)} %get-tuple-element.14.x_ref, f32[16,8,128]{2,1,0:T(8,128)} %get-tuple-element.15.gates_ref, bf16[2,1536,512]{2,1,0:T(8,128)(2,1)} %wg_hbm.1, bf16[2,1536,512]{2,1,0:T(8,128)(2,1)} %wu_hbm.1, bf16[2,512,1536]{2,1,0:T(8,128)(2,1)} %wd_hbm.1, ...), custom_call_target="tpu_custom_call" | custom-call | tf_op jit(solution)/shard_map/experts/pallas_call | solution.py:481
  166.7 1.8 %copy.23 = bf16[128,1536]{1,0:T(8,128)(2,1)} copy(bf16[128,1536]{1,0:T(8,128)(2,1)} %experts.1) | data formatting | bytes 786432
  (7 shorter events, 0.1 us)
